TPU v7x, 32 devices: a whole 2x2x4 slice. The times are simulated.
32 devices in a mesh: groups: 2 (over y), scanx: 4 (over z), scany: 2 (over x), pos: 2 (over core).
Axes of the slice: x: 2, y: 2, z: 4, core: 2. Of those that a mesh axis runs over, the one named last changes fastest.
Arguments:
- specimen: float32 [2, 2048, 512], P(None, ('groups', 'scanx'), 'scany'), parts along dimension 1, may hold values from -5 to 5
- probe_wave: float32 [2, 512, 256], P(None, 'groups'), parts along dimension 1, may hold values from -6 to 6
- amplitudes: bfloat16 [64, 256, 256], P(('groups', 'scanx', 'scany', 'pos')), parts along dimension 0, may hold values from 0 to 2
- offsets: int32 [64, 2], P(('groups', 'scanx', 'scany', 'pos')), parts along dimension 0, may hold values from 0 to 255
Outputs:
- new_specimen: float32 [2, 2048, 512], P(None, ('groups', 'scanx'), 'scany'), parts along dimension 1
- new_probe: float32 [2, 512, 256], P(None, 'groups'), parts along dimension 1
There are 2 independent parts, one for each index of `groups`. A program takes and returns all parts, laid end to end along the dimension named above; each array names one. Nothing has to cross between parts.
Inputs may be any that keep to these rules, and one draw needn't show every extreme that they name: offsets are pixels from the top-left corner of the position's tile.
All inputs are finite; a program needn't handle non-finite values.
Results may differ from a plain program's by a relative error of at most 0.002.
The roundings to bfloat16 on the way count: a program that leaves them out, or rounds other values in their place, can miss the bound.
Values sent between devices are 32-bit elements; how exact they have to be, the bound alone decides.
A program may use at most 64 MiB of HBM per device.

v0:
```python
import math

import jax
import jax.numpy as jnp
from jax import lax
from jax.sharding import PartitionSpec as P


def padded_2(block, sides, width):
    for axis, dim in sides:
        count = lax.axis_size(axis)
        forward = [(i, i + 1) for i in range(count - 1)]
        backward = [(target, source) for source, target in forward]
        low = lax.ppermute(
            lax.slice_in_dim(block, block.shape[dim] - width, None, axis=dim), axis, forward
        )
        high = lax.ppermute(lax.slice_in_dim(block, 0, width, axis=dim), axis, backward)
        block = jnp.concatenate([low, block, high], axis=dim)
    return block


def dft_tables(length):
    positions_index = jnp.arange(length, dtype=jnp.int32)
    phase_index = positions_index[:, None] * positions_index[None, :] % length
    angle_rad = phase_index.astype(jnp.float32) * (2.0 * math.pi / length)
    scale_factor = 1.0 / math.sqrt(length)
    cosine = (jnp.cos(angle_rad) * scale_factor).astype(jnp.bfloat16)
    sine_part = (jnp.sin(angle_rad) * scale_factor).astype(jnp.bfloat16)
    forward_left = jnp.stack(
        [jnp.stack([cosine, sine_part], 1), jnp.stack([-sine_part, cosine], 1)], 0
    )
    forward_right = jnp.stack(
        [jnp.stack([cosine, -sine_part], 1), jnp.stack([sine_part, cosine], 1)], 0
    )
    inverse_left = jnp.stack(
        [jnp.stack([cosine, -sine_part], 1), jnp.stack([sine_part, cosine], 1)], 0
    )
    inverse_right = jnp.stack(
        [jnp.stack([cosine, sine_part], 1), jnp.stack([-sine_part, cosine], 1)], 0
    )
    return (forward_left, forward_right, inverse_left, inverse_right)


def project_exit(patch_wave, probe_real, probe_imag, amplitude, tables):
    forward_left, forward_right, inverse_left, inverse_right = tables
    patch_real = patch_wave[0]
    patch_imag = patch_wave[1]
    exit_real = probe_real * patch_real - probe_imag * patch_imag
    exit_imag = probe_real * patch_imag + probe_imag * patch_real
    exit_wave = jnp.stack([exit_real, exit_imag]).astype(jnp.bfloat16)
    half_done = jnp.einsum(
        "akbr,brv->akv", forward_left, exit_wave, preferred_element_type=jnp.float32
    ).astype(jnp.bfloat16)
    far_field = jnp.einsum(
        "bkv,bval->akl", half_done, forward_right, preferred_element_type=jnp.float32
    )
    magnitude = jnp.sqrt(far_field[0] * far_field[0] + far_field[1] * far_field[1])
    scale_ratio = amplitude.astype(jnp.float32) / jnp.maximum(magnitude, 0.2)
    projected = (far_field * scale_ratio[None]).astype(jnp.bfloat16)
    back_half = jnp.einsum(
        "akbr,brv->akv", inverse_left, projected, preferred_element_type=jnp.float32
    ).astype(jnp.bfloat16)
    back_wave = jnp.einsum(
        "bkv,bval->akl", back_half, inverse_right, preferred_element_type=jnp.float32
    )
    return (back_wave[0] - exit_real, back_wave[1] - exit_imag, patch_real, patch_imag)


def fold_margin(field_in, axis_dim, margin, tile_len):
    extent = field_in.shape[axis_dim]
    inner_part = lax.slice_in_dim(field_in, 2 * margin, 2 * margin + tile_len, axis=axis_dim)
    lower_rim = lax.slice_in_dim(field_in, 0, margin, axis=axis_dim)
    upper_rim = lax.slice_in_dim(field_in, extent - margin, extent, axis=axis_dim)
    lower_widths = [(0, 0)] * field_in.ndim
    upper_widths = [(0, 0)] * field_in.ndim
    lower_widths[axis_dim] = (0, tile_len - margin)
    upper_widths[axis_dim] = (tile_len - margin, 0)
    return inner_part + jnp.pad(lower_rim, lower_widths) + jnp.pad(upper_rim, upper_widths)


def shards(specimen, probe_wave, amplitudes, offsets):
    pattern = probe_wave.shape[1]
    margin = pattern // 2
    tile_len = specimen.shape[1]
    tables = dft_tables(pattern)
    padded = padded_2(specimen, (("scanx", 1), ("scany", 2)), margin)
    probe_real = probe_wave[0]
    probe_imag = probe_wave[1]
    probe_power = probe_real * probe_real + probe_imag * probe_imag
    zero_index = jnp.zeros((), jnp.int32)

    def visit_position(carried, inputs):
        object_grad, probe_grad = carried
        amplitude, offset = inputs
        row_start = offset[0]
        col_start = offset[1]
        patch_wave = lax.dynamic_slice(
            padded, (zero_index, row_start, col_start), (2, pattern, pattern)
        )
        diff_real, diff_imag, patch_real, patch_imag = project_exit(
            patch_wave, probe_real, probe_imag, amplitude, tables
        )
        object_term = jnp.stack(
            [
                probe_real * diff_real + probe_imag * diff_imag,
                probe_real * diff_imag - probe_imag * diff_real,
                probe_power,
            ]
        )
        current = lax.dynamic_slice(
            object_grad, (zero_index, row_start, col_start), (3, pattern, pattern)
        )
        object_grad = lax.dynamic_update_slice(
            object_grad, current + object_term, (zero_index, row_start, col_start)
        )
        probe_term = jnp.stack(
            [
                patch_real * diff_real + patch_imag * diff_imag,
                patch_real * diff_imag - patch_imag * diff_real,
            ]
        )
        return ((object_grad, probe_grad + probe_term), None)

    start_grad = jnp.zeros((3, tile_len + pattern, tile_len + pattern), jnp.float32)
    start_probe = jnp.zeros((2, pattern, pattern), jnp.float32)
    (object_grad, probe_grad), unused = lax.scan(
        visit_position, (start_grad, start_probe), (amplitudes, offsets)
    )
    row_halo = padded_2(object_grad, (("scanx", 1),), margin)
    row_folded = fold_margin(row_halo, 1, margin, tile_len)
    col_halo = padded_2(row_folded, (("scany", 2),), margin)
    core_sum = fold_margin(col_halo, 2, margin, tile_len)
    core_sum = lax.psum(core_sum, "pos")
    new_specimen = specimen + core_sum[0:2] / (core_sum[2:3] + 1.0)
    devices_count = lax.axis_size("scanx") * lax.axis_size("scany") * lax.axis_size("pos")
    step_size = 1.0 / math.sqrt(offsets.shape[0] * devices_count)
    total_grad = lax.psum(probe_grad, ("scanx", "scany", "pos"))
    new_probe = probe_wave + total_grad * step_size
    return (new_specimen, new_probe)


def solution(mesh):
    placed = (
        P(None, ("groups", "scanx"), "scany"),
        P(None, "groups", None),
        P(("groups", "scanx", "scany", "pos"), None, None),
        P(("groups", "scanx", "scany", "pos"), None),
    )
    return jax.shard_map(
        shards,
        mesh=mesh,
        in_specs=placed,
        out_specs=(P(None, ("groups", "scanx"), "scany"), P(None, "groups", None)),
        check_vma=False,
    )
```

profile of v0, /device:TPU:0, one launch (start us, length us, event | category | flops | bytes accessed | tf_op | source)
XLA Modules:
  0.0 249.9 jit_solution(168859406196740415)
XLA Ops:
  7.2 0.0 copy-start.3
  7.2 0.0 all-reduce.9.cloned.1.call-start
  7.2 1.1 fusion.50
  8.3 1.3 collective-permute-start.1
  9.6 5.6 %collective-permute-start = (f32[2,128,256]{2,1,0:T(8,128)S(1)}, f32[2,128,256]{2,1,0:T(8,128)S(1)}, u32[]{:S(2)}, u32[]{:S(2)}) collective-permute-start(f32[2,128,256]{2,1,0:T(8,128)S(1)} %get-tuple-element.187), channel_id=1, source_target_pairs={{0,4},{4,8},{8,12},{1,5},{5,9},{9,13},{2,6},{6,10},{10,14},{3,7},{... | collective-permute-start | bytes 786440 | tf_op jit(solution)/shard_map/ppermute | solution.py:14
  15.2 1.0 fusion.41
  16.2 1.1 multiply_convert_fusion.1
  17.4 0.1 fusion.33
  17.4 0.8 pad_maximum_fusion.2
  18.3 2.5 collective-permute-done
  20.9 0.0 copy-start.1
  20.9 0.9 fusion.49
  21.8 4.4 %collective-permute-start.2 = (f32[2,512,128]{2,1,0:T(8,128)}, f32[2,512,128]{2,1,0:T(8,128)}, u32[]{:S(2)}, u32[]{:S(2)}) collective-permute-start(f32[2,512,128]{2,1,0:T(8,128)} %get-tuple-element.182), channel_id=1, source_target_pairs={{0,2},{1,3},{4,6},{5,7},{8,10},{9,11},{12,14},{13,15},{16,18},{17,... | collective-permute-start | bytes 1572872 | tf_op jit(solution)/shard_map/ppermute | solution.py:14
  26.1 1.3 collective-permute-start.3
  27.4 0.1 pad_maximum_fusion.1
  27.5 0.8 copy.7
  28.3 0.7 multiply_add_fusion.2
  29.0 0.7 slice_bitcast_fusion
  29.8 5.9 %collective-permute-done.2 = f32[2,512,128]{2,1,0:T(8,128)} collective-permute-done((f32[2,512,128]{2,1,0:T(8,128)}, f32[2,512,128]{2,1,0:T(8,128)}, u32[]{:S(2)}, u32[]{:S(2)}) %collective-permute-start.2) | collective-permute-done | bytes 524320 | tf_op jit(solution)/shard_map/ppermute | solution.py:14
  35.7 4.7 %collective-permute-done.3 = f32[2,512,128]{2,1,0:T(8,128)} collective-permute-done((f32[2,512,128]{2,1,0:T(8,128)S(1)}, f32[2,512,128]{2,1,0:T(8,128)}, u32[]{:S(2)}, u32[]{:S(2)}) %collective-permute-start.3) | collective-permute-done | bytes 524320 | tf_op jit(solution)/shard_map/ppermute | solution.py:17
  40.4 1.4 pad_maximum_fusion
  41.8 0.0 copy-start.5
  41.8 2.0 broadcast_in_dim.10
  43.8 53.0 %while.14 = (s32[]{:T(128)}, f32[3,512,512]{2,1,0:T(8,128)}, f32[2,256,256]{2,1,0:T(8,128)}, s32[2,2]{1,0:T(2,128)S(1)}, f32[256,256]{1,0:T(8,128)}, /*index=5*/...) while((s32[]{:T(128)}, f32[3,512,512]{2,1,0:T(8,128)}, ...), condition=%wide.region_1.2_spmd.clone, body=%wide.region_0.1_spmd.clone.sunk | while | flops 540737536 | bytes 17170760 | solution.py:126
  43.8 0.6 fusion.71
  48.2 2.0 fusion.72
  50.1 1.9 convolution_bitcast_fusion.6
  52.0 1.8 fusion.73
  53.8 2.0 convolution_bitcast_fusion.7
  55.8 1.3 multiply_add_fusion.4
  57.1 1.2 fusion.74
  58.3 0.9 maximum_add_fusion.5
  59.1 1.7 maximum_add_fusion.4
  60.8 8.7 %dynamic_update_slice.6 = f32[3,512,512]{2,1,0:T(8,128)} dynamic-update-slice(f32[3,512,512]{2,1,0:T(8,128)} %get-tuple-element.303, f32[3,256,256]{2,1,0:T(8,128)S(1)} %maximum_add_fusion.4, s32[]{:T(128)} %constant.39.clone.1..sunk, s32[]{:T(128)S(6)} %select_n.64, s32[]{:T(128)S(6)} %select_n.65) | dynamic-update-slice | bytes 1572868 | tf_op jit(solution)/shard_map/while/body/eval_jaxpr/dynamic_update_slice | solution.py:113
  69.5 0.6 fusion.71
  73.9 2.0 fusion.72
  75.8 1.9 convolution_bitcast_fusion.6
  77.7 1.8 fusion.73
  79.5 2.0 convolution_bitcast_fusion.7
  81.5 1.3 multiply_add_fusion.4
  82.7 1.2 fusion.74
  83.9 1.9 maximum_add_fusion.5
  85.8 1.7 maximum_add_fusion.4
  87.5 9.3 %dynamic_update_slice.6 = f32[3,512,512]{2,1,0:T(8,128)} dynamic-update-slice(f32[3,512,512]{2,1,0:T(8,128)} %get-tuple-element.303, f32[3,256,256]{2,1,0:T(8,128)S(1)} %maximum_add_fusion.4, s32[]{:T(128)} %constant.39.clone.1..sunk, s32[]{:T(128)S(6)} %select_n.64, s32[]{:T(128)S(6)} %select_n.65) | dynamic-update-slice | bytes 1572868 | tf_op jit(solution)/shard_map/while/body/eval_jaxpr/dynamic_update_slice | solution.py:113
  96.8 1.6 fusion.47
  98.5 3.2 %collective-permute-start.4 = (f32[3,128,512]{2,1,0:T(8,128)S(1)}, f32[3,128,512]{2,1,0:T(8,128)S(1)}, u32[]{:S(2)}, u32[]{:S(2)}) collective-permute-start(f32[3,128,512]{2,1,0:T(8,128)S(1)} %get-tuple-element.178), channel_id=1, source_target_pairs={{0,4},{4,8},{8,12},{1,5},{5,9},{9,13},{2,6},{6,10},{10,14},{3,7},{... | collective-permute-start | bytes 2359304 | tf_op jit(solution)/shard_map/ppermute | solution.py:14
  101.7 1.3 collective-permute-start.5
  103.0 15.0 %collective-permute-done.4 = f32[3,128,512]{2,1,0:T(8,128)S(1)} collective-permute-done((f32[3,128,512]{2,1,0:T(8,128)S(1)}, f32[3,128,512]{2,1,0:T(8,128)S(1)}, u32[]{:S(2)}, u32[]{:S(2)}) %collective-permute-start.4) | collective-permute-done | bytes 786464 | tf_op jit(solution)/shard_map/ppermute | solution.py:14
  118.0 4.2 %collective-permute-done.5 = f32[3,128,512]{2,1,0:T(8,128)S(1)} collective-permute-done((f32[3,128,512]{2,1,0:T(8,128)S(1)}, f32[3,128,512]{2,1,0:T(8,128)S(1)}, u32[]{:S(2)}, u32[]{:S(2)}) %collective-permute-start.5) | collective-permute-done | bytes 786464 | tf_op jit(solution)/shard_map/ppermute | solution.py:17
  122.2 0.3 pad_add_fusion
  122.5 0.9 fusion.48
  123.4 1.4 collective-permute-start.6
  124.9 1.3 collective-permute-start.7
  126.2 0.0 all-reduce.9.cloned.1.call-update
  126.2 0.0 all-reduce.7.cloned.1.call-start
  126.3 5.0 %collective-permute-done.6 = f32[3,256,128]{2,1,0:T(8,128)S(1)} collective-permute-done((f32[3,256,128]{2,1,0:T(8,128)}, f32[3,256,128]{2,1,0:T(8,128)S(1)}, u32[]{:S(2)}, u32[]{:S(2)}) %collective-permute-start.6) | collective-permute-done | bytes 393248 | tf_op jit(solution)/shard_map/ppermute | solution.py:14
  131.3 4.5 %collective-permute-done.7 = f32[3,256,128]{2,1,0:T(8,128)S(1)} collective-permute-done((f32[3,256,128]{2,1,0:T(8,128)}, f32[3,256,128]{2,1,0:T(8,128)S(1)}, u32[]{:S(2)}, u32[]{:S(2)}) %collective-permute-start.7) | collective-permute-done | bytes 393248 | tf_op jit(solution)/shard_map/ppermute | solution.py:17
  135.8 1.1 fusion.28
  136.8 0.0 all-reduce.7.cloned.1.call-update
  136.9 81.5 %all-reduce.9.cloned.1.call-done = f32[2,256,256]{2,1,0:T(8,128)} async-done(((f32[2,256,256]{2,1,0:T(8,128)}), f32[2,256,256]{2,1,0:T(8,128)}) %all-reduce.9.cloned.1.call-update) | async-done | bytes 524304 | tf_op jit(solution)/shard_map/psum | solution.py:137
  218.3 1.9 multiply_add_fusion.1
  220.2 19.9 %all-reduce.7.cloned.1.call-done = f32[3,256,256]{2,1,0:T(8,128)} async-done(((f32[3,256,256]{2,1,0:T(8,128)}), f32[3,256,256]{2,1,0:T(8,128)}) %all-reduce.7.cloned.1.call-update) | async-done | bytes 786448 | tf_op jit(solution)/shard_map/psum | solution.py:133
  240.1 1.0 fusion.37
  241.1 1.9 fusion.29
  (16 shorter events, 0.1 us)
Async XLA Ops:
  7.2 13.6 %copy-start.3 = (f32[2,256,256]{2,1,0:T(8,128)S(1)}, f32[2,256,256]{2,1,0:T(8,128)}, u32[]{:S(2)}) copy-start(f32[2,256,256]{2,1,0:T(8,128)} %param.6) | copy-start | bytes 1572868
  7.2 211.1 %all-reduce.9.cloned.1.call-start = ((), (), s32[]{:S(2)}) async-start(), calls=%async_computation.1 | async-start | bytes 1048576 | tf_op jit(solution)/shard_map/psum | solution.py:137
  8.3 12.5 %collective-permute-start.1 = (f32[2,128,256]{2,1,0:T(8,128)S(1)}, f32[2,128,256]{2,1,0:T(8,128)S(1)}, u32[]{:S(2)}, u32[]{:S(2)}) collective-permute-start(f32[2,128,256]{2,1,0:T(8,128)S(1)} %get-tuple-element.186), channel_id=1, source_target_pairs={{4,0},{8,4},{12,8},{5,1},{9,5},{13,9},{6,2},{10,6},{14,10},{7,3},{... | collective-permute-start | bytes 786440 | tf_op jit(solution)/shard_map/ppermute | solution.py:17
  9.6 11.1 %collective-permute-start = (f32[2,128,256]{2,1,0:T(8,128)S(1)}, f32[2,128,256]{2,1,0:T(8,128)S(1)}, u32[]{:S(2)}, u32[]{:S(2)}) collective-permute-start(f32[2,128,256]{2,1,0:T(8,128)S(1)} %get-tuple-element.187), channel_id=1, source_target_pairs={{0,4},{4,8},{8,12},{1,5},{5,9},{9,13},{2,6},{6,10},{10,14},{3,7},{... | collective-permute-start | bytes 786440 | tf_op jit(solution)/shard_map/ppermute | solution.py:14
  20.9 7.4 %copy-start.1 = (f32[2,256,256]{2,1,0:T(8,128)S(1)}, f32[2,256,256]{2,1,0:T(8,128)}, u32[]{:S(2)}) copy-start(f32[2,256,256]{2,1,0:T(8,128)} %param.7) | copy-start | bytes 1572868
  21.8 13.9 %collective-permute-start.2 = (f32[2,512,128]{2,1,0:T(8,128)}, f32[2,512,128]{2,1,0:T(8,128)}, u32[]{:S(2)}, u32[]{:S(2)}) collective-permute-start(f32[2,512,128]{2,1,0:T(8,128)} %get-tuple-element.182), channel_id=1, source_target_pairs={{0,2},{1,3},{4,6},{5,7},{8,10},{9,11},{12,14},{13,15},{16,18},{17,... | collective-permute-start | bytes 1572872 | tf_op jit(solution)/shard_map/ppermute | solution.py:14
  26.1 14.2 %collective-permute-start.3 = (f32[2,512,128]{2,1,0:T(8,128)S(1)}, f32[2,512,128]{2,1,0:T(8,128)}, u32[]{:S(2)}, u32[]{:S(2)}) collective-permute-start(f32[2,512,128]{2,1,0:T(8,128)S(1)} %get-tuple-element.183), channel_id=1, source_target_pairs={{2,0},{3,1},{6,4},{7,5},{10,8},{11,9},{14,12},{15,13},{18,16},{19,... | collective-permute-start | bytes 1572872 | tf_op jit(solution)/shard_map/ppermute | solution.py:17
  41.8 2.0 copy-start.5
  96.8 25.4 %copy-start = (f32[3,512,512]{2,1,0:T(8,128)S(1)}, f32[3,512,512]{2,1,0:T(8,128)}, u32[]{:S(2)}) copy-start(f32[3,512,512]{2,1,0:T(8,128)} %get-tuple-element.93) | copy-start | bytes 9437188
  98.5 19.5 %collective-permute-start.4 = (f32[3,128,512]{2,1,0:T(8,128)S(1)}, f32[3,128,512]{2,1,0:T(8,128)S(1)}, u32[]{:S(2)}, u32[]{:S(2)}) collective-permute-start(f32[3,128,512]{2,1,0:T(8,128)S(1)} %get-tuple-element.178), channel_id=1, source_target_pairs={{0,4},{4,8},{8,12},{1,5},{5,9},{9,13},{2,6},{6,10},{10,14},{3,7},{... | collective-permute-start | bytes 2359304 | tf_op jit(solution)/shard_map/ppermute | solution.py:14
  101.7 20.5 %collective-permute-start.5 = (f32[3,128,512]{2,1,0:T(8,128)S(1)}, f32[3,128,512]{2,1,0:T(8,128)S(1)}, u32[]{:S(2)}, u32[]{:S(2)}) collective-permute-start(f32[3,128,512]{2,1,0:T(8,128)S(1)} %get-tuple-element.179), channel_id=1, source_target_pairs={{4,0},{8,4},{12,8},{5,1},{9,5},{13,9},{6,2},{10,6},{14,10},{7,3},{... | collective-permute-start | bytes 2359304 | tf_op jit(solution)/shard_map/ppermute | solution.py:17
  123.4 94.9 %copy-start.2 = (f32[2,256,256]{2,1,0:T(8,128)S(1)}, f32[2,256,256]{2,1,0:T(8,128)}, u32[]{:S(2)}) copy-start(f32[2,256,256]{2,1,0:T(8,128)} %param.7) | copy-start | bytes 1572868
  123.4 7.8 %collective-permute-start.6 = (f32[3,256,128]{2,1,0:T(8,128)}, f32[3,256,128]{2,1,0:T(8,128)S(1)}, u32[]{:S(2)}, u32[]{:S(2)}) collective-permute-start(f32[3,256,128]{2,1,0:T(8,128)} %get-tuple-element.180), channel_id=1, source_target_pairs={{0,2},{1,3},{4,6},{5,7},{8,10},{9,11},{12,14},{13,15},{16,18},{17,... | collective-permute-start | bytes 1179656 | tf_op jit(solution)/shard_map/ppermute | solution.py:14
  124.9 10.9 %collective-permute-start.7 = (f32[3,256,128]{2,1,0:T(8,128)}, f32[3,256,128]{2,1,0:T(8,128)S(1)}, u32[]{:S(2)}, u32[]{:S(2)}) collective-permute-start(f32[3,256,128]{2,1,0:T(8,128)} %get-tuple-element.181), channel_id=1, source_target_pairs={{2,0},{3,1},{6,4},{7,5},{10,8},{11,9},{14,12},{15,13},{18,16},{19,... | collective-permute-start | bytes 1179656 | tf_op jit(solution)/shard_map/ppermute | solution.py:17
  126.2 114.9 %copy-start.4 = (f32[2,256,256]{2,1,0:T(8,128)S(1)}, f32[2,256,256]{2,1,0:T(8,128)}, u32[]{:S(2)}) copy-start(f32[2,256,256]{2,1,0:T(8,128)} %param.6) | copy-start | bytes 1572868
  126.2 113.9 %all-reduce.7.cloned.1.call-start = ((), (), s32[]{:S(2)}) async-start(), calls=%async_computation | async-start | bytes 1572864 | tf_op jit(solution)/shard_map/psum | solution.py:133
Sparse Core Ops, SparseCore 0:
  126.3 91.9 all-reduce.8
  220.7 19.4 all-reduce.6
where the time goes:
time: 251 us; the launch traced here: 250 us
  waiting for transfers between devices  143 us (57%)
  other arithmetic  29.9 us (12%)
  local copies, waits for them, and re-layouts  27.4 us (11%)
  starting transfers between devices  19.8 us (8%)
  between operations  14.2 us (6%)
  matrix products  7.75 us (3%)
  loops' own time  7.59 us (3%)
    psum x1, waiting for transfers between devices, shards(): total_grad = lax.psum(probe_grad, ('scanx', 'scany', 'pos'))  81.5 us
    ppermute x4, waiting for transfers between devices, padded_2(): lax.ppermute(lax.slice_in_dim(block, block.shape[dim] - width, None, axis...  28.4 us
    psum x1, waiting for transfers between devices, shards(): core_sum = lax.psum(core_sum, 'pos')  19.9 us
    dynamic_update_slice x2, local copies, waits for them, and re-layouts, visit_position(): lax.dynamic_update_slice(object_grad, current + object_term, (zero_index,...  18 us
    ppermute x4, starting transfers between devices, padded_2(): lax.ppermute(lax.slice_in_dim(block, block.shape[dim] - width, None, axis...  14.6 us
    ppermute x4, waiting for transfers between devices, padded_2(): lax.ppermute(lax.slice_in_dim(block, 0, width, axis=dim), axis, backward)  13.4 us
    another operation x1, loops' own time, shards(): lax.scan(visit_position, (start_grad, start_probe), (amplitudes, offsets))  7.59 us
    ppermute x4, starting transfers between devices, padded_2(): lax.ppermute(lax.slice_in_dim(block, 0, width, axis=dim), axis, backward)  5.16 us
  transfers between devices with their start and end apart: 10, of which 9 were waited for; matrix products, arithmetic and copies ran while one was open for 3% of the time, Pallas kernels for 0%

commit v1 on v0

v1 whole, which is shorter than its diff:
```python
import functools
import math

import jax
import jax.numpy as jnp
import numpy as np
from jax import lax
from jax.experimental import pallas as pl
from jax.experimental.pallas import tpu as pltpu
from jax.sharding import PartitionSpec as P

MESH = pl.DeviceIdType.MESH
VMEM = pltpu.VMEM


def remote(src, dst, send, recv, where):
    return pltpu.make_async_remote_copy(
        src_ref=src, dst_ref=dst, send_sem=send, recv_sem=recv, device_id=where, device_id_type=MESH
    )


def greet(conditions_devices):
    barrier = pltpu.get_barrier_semaphore()
    for present, where in conditions_devices:
        if present is True:
            pl.semaphore_signal(barrier, inc=1, device_id=where, device_id_type=MESH)
        else:

            @pl.when(present)
            def _(where=where):
                pl.semaphore_signal(barrier, inc=1, device_id=where, device_id_type=MESH)

    fixed = sum(1 for present, _ in conditions_devices if present is True)
    peers = [present.astype(jnp.int32) for present, _ in conditions_devices if present is not True]
    pl.semaphore_wait(barrier, sum(peers, fixed))


class Side:
    def __init__(self, axis, count, step):
        me = lax.axis_index(axis)
        self.has = me > 0 if step < 0 else me < count - 1
        self.where = {axis: me + step}


def halo_kernel(nx, ny, spec, pad, send, recv):
    tile = spec.shape[1]
    half = (pad.shape[1] - tile) // 2
    p = lax.axis_index("pos")
    partner = {"pos": 1 - p}
    up, down = Side("scanx", nx, -1), Side("scanx", nx, 1)
    left, right = Side("scany", ny, -1), Side("scany", ny, 1)
    greet([(True, partner)] + [(s.has, s.where) for s in (up, down, left, right)])
    own = pl.ds(half, tile)
    low, high = pl.ds(0, half), pl.ds(half + tile, half)
    every = pl.ds(0, tile + 2 * half)
    first, last = pl.ds(half, half), pl.ds(tile, half)

    def role(q, sides1, sides2, rows_first):
        def at1(piece):
            return (q, piece, own) if rows_first else (q, own, piece)

        def at2(piece):
            return (q, every, piece) if rows_first else (q, piece, every)

        def src1(k):
            piece = pl.ds(0, half) if k == 0 else pl.ds(tile - half, half)
            return spec.at[q, piece, :] if rows_first else spec.at[q, :, piece]

        copies1 = [
            remote(src1(k), pad.at[at1(high if k == 0 else low)], send.at[k], recv.at[k], sides1[k].where)
            for k in range(2)
        ]
        for k in range(2):
            pl.when(sides1[k].has)(copies1[k].start)
        pad[:, own, own] = spec[...]
        for k in range(2):
            mine = low if k == 0 else high

            @pl.when(jnp.logical_not(sides1[k].has))
            def _():
                pad[at1(mine)] = jnp.zeros(pad.at[at1(mine)].shape, pad.dtype)

            @pl.when(jnp.logical_not(sides2[k].has))
            def _():
                pad[at2(mine)] = jnp.zeros(pad.at[at2(mine)].shape, pad.dtype)

        for k in range(2):
            pl.when(sides1[1 - k].has)(copies1[k].wait_recv)
        copies2 = [
            remote(
                pad.at[at2(first if k == 0 else last)],
                pad.at[at2(high if k == 0 else low)],
                send.at[2 + k],
                recv.at[2 + k],
                sides2[k].where,
            )
            for k in range(2)
        ]
        for k in range(2):
            pl.when(sides2[k].has)(copies2[k].start)
        share1 = [
            remote(pad.at[at1(m)], pad.at[at1(m)], send.at[4 + k], recv.at[4 + k], partner)
            for k, m in enumerate((low, high))
        ]
        for c in share1:
            c.start()
        share2 = [
            remote(pad.at[at2(m)], pad.at[at2(m)], send.at[6 + k], recv.at[6 + k], partner)
            for k, m in enumerate((low, high))
        ]
        for k in range(2):
            pl.when(sides2[k].has)(copies2[1 - k].wait_recv)
            share2[k].start()
        for k in range(2):
            pl.when(sides1[k].has)(copies1[k].wait_send)
            pl.when(sides2[k].has)(copies2[k].wait_send)
        for c in share1 + share2:
            c.wait_send()

    def arriving(q, rows_first):
        def at1(piece):
            return (q, piece, own) if rows_first else (q, own, piece)

        def at2(piece):
            return (q, every, piece) if rows_first else (q, piece, every)

        for k, m in enumerate((low, high)):
            remote(pad.at[at1(m)], pad.at[at1(m)], send.at[4 + k], recv.at[4 + k], partner).wait_recv()
        for k, m in enumerate((low, high)):
            remote(pad.at[at2(m)], pad.at[at2(m)], send.at[6 + k], recv.at[6 + k], partner).wait_recv()

    @pl.when(p == 0)
    def _():
        role(0, (left, right), (up, down), False)
        arriving(1, True)

    @pl.when(p == 1)
    def _():
        role(1, (up, down), (left, right), True)
        arriving(0, False)


def dot(a, b):
    return jnp.dot(a, b, preferred_element_type=jnp.float32)


def step_kernel(offsets, pad, probe, amplitudes, table_a, table_b, grad, probe_grad):
    m = probe.shape[1]
    tall, span = m + 8, m + 128
    pr, pi = probe[0], probe[1]
    power = pr * pr + pi * pi
    grad[...] = jnp.zeros(grad.shape, grad.dtype)
    blank_rows = jnp.zeros((tall - m, m), jnp.float32)
    blank_cols = jnp.zeros((tall, span - m), jnp.float32)
    bf = jnp.bfloat16
    sum_r = sum_i = None
    for j in range(amplitudes.shape[0]):
        row, col = offsets[j, 0], offsets[j, 1]
        row_in, col_in = lax.rem(row, 8), lax.rem(col, 128)
        rows = pl.ds(pl.multiple_of(row - row_in, 8), tall)
        cols = pl.ds(pl.multiple_of(col - col_in, 128), span)

        def window(k):
            block = pad[k, rows, cols]
            block = pltpu.roll(block, lax.rem(span - col_in, span), 1)[:, :m]
            return pltpu.roll(block, lax.rem(tall - row_in, tall), 0)[:m]

        ar, ai = window(0), window(1)
        er = pr * ar - pi * ai
        ei = pr * ai + pi * ar
        half = dot(table_a[...], jnp.concatenate([er.astype(bf), ei.astype(bf)], 0)).astype(bf)
        far = dot(jnp.concatenate([half[:m], half[m:]], 1), table_b[...])
        fr, fi = far[:, :m], far[:, m:]
        ratio = amplitudes[j].astype(jnp.float32) / jnp.maximum(jnp.sqrt(fr * fr + fi * fi), 0.2)
        projected = jnp.concatenate([(fr * ratio).astype(bf), (fi * ratio).astype(bf)], 0)
        back_half = dot(table_b[...], projected).astype(bf)
        back = dot(jnp.concatenate([back_half[:m], back_half[m:]], 1), table_a[...])
        dr = back[:, :m] - er
        di = back[:, m:] - ei
        for k, term in enumerate((pr * dr + pi * di, pr * di - pi * dr, power)):
            moved = pltpu.roll(jnp.concatenate([term, blank_rows], 0), row_in, 0)
            moved = pltpu.roll(jnp.concatenate([moved, blank_cols], 1), col_in, 1)
            grad[k, rows, cols] = grad[k, rows, cols] + moved
        tr = ar * dr + ai * di
        ti = ar * di - ai * dr
        sum_r = tr if sum_r is None else sum_r + tr
        sum_i = ti if sum_i is None else sum_i + ti
    lanes = probe_grad.shape[2]
    for k, value in enumerate((sum_r, sum_i)):
        for h in range(m // lanes):
            probe_grad[k, h * m : (h + 1) * m, :] = value[:, h * lanes : (h + 1) * lanes]


def reduce_kernel(
    nx, ny, grad, prob, core, total, pair, acc, zr1, xr1, zr2, xr2, ppair, pacc, pr1, pr2, send, recv, psend, precv
):
    w = grad.shape[-1]
    q4 = w // 4
    p = lax.axis_index("pos")
    partner = {"pos": 1 - p}
    up, down = Side("scanx", nx, -1), Side("scanx", nx, 1)
    left, right = Side("scany", ny, -1), Side("scany", ny, 1)
    mx, my = lax.axis_index("scanx"), lax.axis_index("scany")
    greet(
        [(True, partner)]
        + [(True, {"scanx": lax.rem(mx + d, nx)}) for d in range(1, nx)]
        + [(True, {"scany": lax.rem(my + d, ny)}) for d in range(1, ny)]
    )

    def role(q, axis1, n1, axis2, n2, sides1, sides2, rows_first):
        o = 1 - q
        me1, me2 = lax.axis_index(axis1), lax.axis_index(axis2)
        c_prob = remote(prob.at[o], ppair, psend.at[0, 0], precv.at[0, 0], partner)
        c_prob.start()
        c_ch = remote(grad.at[o], pair.at[:, 0:2], send.at[0], recv.at[0], partner)
        c_ill = remote(grad.at[2, :, o], pair.at[:, 2], send.at[1], recv.at[1], partner)
        c_ch.start()
        c_ill.start()

        def scatter(stage, n, axis, me, src, size, landing):
            out = []
            for d in range(1, n):
                j = lax.rem(me + d, n)
                out.append(
                    remote(
                        src.at[pl.ds(j * size, size)],
                        landing.at[pl.ds(d * size, size)],
                        psend.at[stage, d],
                        precv.at[stage, d],
                        {axis: j},
                    )
                )
            for c in out:
                c.start()
            return out

        def gather(stage, n, axis, me, piece):
            out = []
            for d in range(1, n):
                out.append(
                    remote(
                        total.at[q, piece],
                        total.at[q, piece],
                        psend.at[stage, d],
                        precv.at[stage, d],
                        {axis: lax.rem(me + d, n)},
                    )
                )
            for c in out:
                c.start()
            return out

        c_prob.wait_recv()
        pacc[...] = prob[q] + ppair[...]
        c1 = scatter(1, n1, axis1, me1, pacc, n2, pr1)

        c_ch.wait_recv()
        c_ill.wait_recv()
        acc[:, 0:2] = grad[q] + pair[:, 0:2]
        acc[:, 2] = grad[2, :, q] + pair[:, 2]
        rim1 = zr1 if rows_first else xr1
        rim2 = xr2 if rows_first else zr2
        if rows_first:
            src1 = [acc.at[0], acc.at[3]]
            src2 = [acc.at[1:3, :, :, 0:q4], acc.at[1:3, :, :, 3 * q4 : w]]
        else:
            src1 = [acc.at[:, :, :, 0:q4], acc.at[:, :, :, 3 * q4 : w]]
            src2 = [acc.at[0, :, :, q4 : 3 * q4], acc.at[3, :, :, q4 : 3 * q4]]

        def fold(k, rim, rows, inner):
            if rows:
                g = 2 if k == 0 else 1
                cols = pl.ds(q4, 2 * q4) if inner else pl.ds(0, w)
                acc[g, :, :, cols] = acc[g, :, :, cols] + rim[k]
            else:
                cols = pl.ds(2 * q4, q4) if k == 0 else pl.ds(q4, q4)
                groups = pl.ds(1, 2) if inner else pl.ds(0, 4)
                acc[groups, :, :, cols] = acc[groups, :, :, cols] + rim[k]

        g1 = [remote(src1[k], rim1.at[k], send.at[2 + k], recv.at[2 + k], sides1[k].where) for k in range(2)]
        for k in range(2):
            pl.when(sides1[k].has)(g1[k].start)

        for c in c1:
            c.wait_recv()
        mine = pacc[pl.ds(me1 * n2, n2)]
        for d in range(1, n1):
            mine = mine + pr1[d * n2 : (d + 1) * n2]
        p1 = ppair
        p1[0:n2] = mine
        c2 = scatter(2, n2, axis2, me2, p1, 1, pr2)

        for k in range(2):

            @pl.when(sides1[1 - k].has)
            def _():
                g1[k].wait_recv()
                fold(k, rim1, rows_first, False)

        g2 = [remote(src2[k], rim2.at[k], send.at[4 + k], recv.at[4 + k], sides2[k].where) for k in range(2)]
        for k in range(2):
            pl.when(sides2[k].has)(g2[k].start)

        for c in c2:
            c.wait_recv()
        one = p1[pl.ds(me2, 1)]
        for d in range(1, n2):
            one = one + pr2[d : d + 1]
        total[q, pl.ds(me1 * n2 + me2, 1)] = one
        c3 = gather(3, n2, axis2, me2, pl.ds(me1 * n2 + me2, 1))

        for k in range(2):

            @pl.when(sides2[1 - k].has)
            def _():
                g2[k].wait_recv()
                fold(k, rim2, not rows_first, True)

        core[q] = acc[1:3, :, :, q4 : 3 * q4]
        c_core = remote(core.at[q], core.at[q], send.at[6], recv.at[6], partner)
        c_core.start()
        for c in c3:
            c.wait_recv()
        c4 = gather(4, n1, axis1, me1, pl.ds(me1 * n2, n2))
        for c in c4:
            c.wait_recv()
        c_tot = remote(total.at[q], total.at[q], psend.at[5, 0], precv.at[5, 0], partner)
        c_tot.start()
        for k in range(2):
            pl.when(sides1[k].has)(g1[k].wait_send)
            pl.when(sides2[k].has)(g2[k].wait_send)
        for c in [c_prob, c_ch, c_ill] + c1 + c2 + c3 + c4 + [c_core, c_tot]:
            c.wait_send()
        remote(core.at[o], core.at[o], send.at[6], recv.at[6], partner).wait_recv()
        remote(total.at[o], total.at[o], psend.at[5, 0], precv.at[5, 0], partner).wait_recv()

    @pl.when(p == 0)
    def _():
        role(0, "scany", ny, "scanx", nx, (left, right), (up, down), False)

    @pl.when(p == 1)
    def _():
        role(1, "scanx", nx, "scany", ny, (up, down), (left, right), True)


def tables(length):
    index = np.arange(length)
    angle = ((index[:, None] * index[None, :]) % length).astype(np.float32) * np.float32(2.0 * math.pi / length)
    scale = np.float32(1.0 / math.sqrt(length))
    c = np.cos(angle) * scale
    s = np.sin(angle) * scale
    a = np.block([[c, s], [-s, c]]).astype(jnp.bfloat16)
    b = np.block([[c, -s], [s, c]]).astype(jnp.bfloat16)
    return a, b


def shards(nx, ny, consts, specimen, probe_wave, amplitudes, offsets):
    m = probe_wave.shape[1]
    tile = specimen.shape[1]
    wide = tile + m
    f32 = jnp.float32
    vm = pl.BlockSpec(memory_space=VMEM)
    sm = pl.BlockSpec(memory_space=pltpu.SMEM)
    dma = pltpu.SemaphoreType.DMA
    pad = pl.pallas_call(
        functools.partial(halo_kernel, nx, ny),
        out_shape=jax.ShapeDtypeStruct((2, wide, wide), f32),
        in_specs=[vm],
        out_specs=vm,
        scratch_shapes=[dma((8,)), dma((8,))],
        compiler_params=pltpu.CompilerParams(collective_id=0, has_side_effects=True),
        name="halo",
    )(specimen)
    lanes = 128
    units = m * m // lanes
    grad, probe_grad = pl.pallas_call(
        step_kernel,
        out_shape=[
            jax.ShapeDtypeStruct((3, wide, wide), f32),
            jax.ShapeDtypeStruct((2, units, lanes), f32),
        ],
        in_specs=[sm] + [vm] * 5,
        out_specs=[vm, vm],
        name="step",
    )(offsets, pad, probe_wave, amplitudes, consts[0], consts[1])
    n = nx * ny
    s = units // n
    h = wide // 8
    most = max(nx, ny)
    core, total = pl.pallas_call(
        functools.partial(reduce_kernel, nx, ny),
        out_shape=[
            jax.ShapeDtypeStruct((2, 2, 3, h, wide // 2), f32),
            jax.ShapeDtypeStruct((2, n, s, lanes), f32),
        ],
        in_specs=[vm, vm],
        out_specs=[vm, vm],
        scratch_shapes=[
            VMEM((4, 3, h, wide), f32),
            VMEM((4, 3, h, wide), f32),
            VMEM((2, 3, h, wide), f32),
            VMEM((2, 4, 3, h, wide // 4), f32),
            VMEM((2, 3, h, wide // 2), f32),
            VMEM((2, 2, 3, h, wide // 4), f32),
            VMEM((n, s, lanes), f32),
            VMEM((n, s, lanes), f32),
            VMEM((n, s, lanes), f32),
            VMEM((most, s, lanes), f32),
            dma((7,)),
            dma((7,)),
            dma((6, most)),
            dma((6, most)),
        ],
        compiler_params=pltpu.CompilerParams(collective_id=1, has_side_effects=True),
        name="reduce",
    )(grad.reshape(3, 4, 2, h, wide), probe_grad.reshape(2, n, s, lanes))
    parts = core[:, :, 0:2].reshape(2, tile, tile)
    light = core[:, :, 2].transpose(1, 0, 2, 3).reshape(tile, tile)
    new_specimen = specimen + parts / (light[None] + 1.0)
    step_size = 1.0 / math.sqrt(offsets.shape[0] * n * 2)
    summed = total.reshape(2, m // lanes, m, lanes).transpose(0, 2, 1, 3).reshape(2, m, m)
    return new_specimen, probe_wave + summed * step_size


def solution(mesh):
    nx, ny = mesh.shape["scanx"], mesh.shape["scany"]

    def run(specimen, probe_wave, amplitudes, offsets):
        consts = tables(probe_wave.shape[2])
        return jax.shard_map(
            lambda *args: shards(nx, ny, [jnp.asarray(t) for t in consts], *args),
            mesh=mesh,
            in_specs=(
                P(None, ("groups", "scanx"), "scany"),
                P(None, "groups", None),
                P(("groups", "scanx", "scany", "pos"), None, None),
                P(("groups", "scanx", "scany", "pos"), None),
            ),
            out_specs=(P(None, ("groups", "scanx"), "scany"), P(None, "groups", None)),
            check_vma=False,
        )(specimen, probe_wave, amplitudes, offsets)

    return run
```

time: 251 us -> 58 us (0.23)
  waiting for transfers between devices: 143 us -> 0 us
  Pallas kernels: 0 us -> 52.7 us
  other arithmetic: 29.9 us -> 3.18 us
  local copies, waits for them, and re-layouts: 27.4 us -> 1.11 us
  starting transfers between devices: 19.8 us -> 0 us
  between operations: 14.2 us -> 0.68 us
  matrix products: 7.75 us -> 0 us
  loops' own time: 7.59 us -> 0 us
    psum x2 -> x0, waiting for transfers between devices: 101 us -> none  [the longest x1 81.5 us: shards(): total_grad = lax.psum(probe_grad, ('scanx', 'scany', 'pos'))]
    pallas_call x0 -> x3, Pallas kernels: none -> 52.7 us  [the longest x1 27.7 us: shards(): pl.pallas_call(functools.partial(reduce_kernel, nx, ny), out_shape=[jax.S...]
    ppermute x8 -> x0, waiting for transfers between devices: 41.7 us -> none  [the longest x4 28.4 us: padded_2(): lax.ppermute(lax.slice_in_dim(block, block.shape[dim] - width, None, axis...]
    ppermute x8 -> x0, starting transfers between devices: 19.8 us -> none  [the longest x4 14.6 us: padded_2(): lax.ppermute(lax.slice_in_dim(block, block.shape[dim] - width, None, axis...]
    dynamic_update_slice x2 -> x0, local copies, waits for them, and re-layouts: 18 us -> none  [visit_position(): lax.dynamic_update_slice(object_grad, current + object_term, (zero_index,...]
    add x13 -> x2, other arithmetic: 17 us -> 2.09 us  [the longest x1 1.12 us: shards(): return (new_specimen, probe_wave + summed * step_size)]
    dot_general x4 -> x0, matrix products: 7.75 us -> none  [the longest x2 3.96 us: project_exit(): jnp.einsum('bkv,bval->akl', back_half, inverse_right, preferred_element_t...]
    another operation x1 -> x0, loops' own time: 7.59 us -> none  [shards(): lax.scan(visit_position, (start_grad, start_probe), (amplitudes, offsets))]
  transfers between devices with their start and end apart: 10 -> 0, of which waited for: 9 -> 0; matrix products, arithmetic and copies ran while one was open for 3% -> 0% of each run, Pallas kernels for 0% -> 0%
where the time goes in v1:
time: 58 us; the launch traced here: 57.7 us
  Pallas kernels  52.7 us (91%)
  other arithmetic  3.18 us (5%)
  local copies, waits for them, and re-layouts  1.11 us (2%)
  between operations  0.68 us (1%)
    pallas_call x1, Pallas kernels, shards(): pl.pallas_call(functools.partial(reduce_kernel, nx, ny), out_shape=[jax.S...  27.7 us
    pallas_call x1, Pallas kernels, shards(): pl.pallas_call(functools.partial(halo_kernel, nx, ny), out_shape=jax.Shap...  17.1 us
    pallas_call x1, Pallas kernels, shards(): pl.pallas_call(step_kernel, out_shape=[jax.ShapeDtypeStruct((3, wide, wid...  7.91 us

profile of v1, /device:TPU:0, one launch (start us, length us, event | category | flops | bytes accessed | tf_op | source)
XLA Modules:
  0.0 57.7 jit_solution(15739710316219208011)
XLA Ops:
  0.6 17.1 %halo.1.pad = f32[2,512,512]{2,1,0:T(8,128)} custom-call(f32[2,256,256]{2,1,0:T(8,128)} %spec.1), custom_call_target="tpu_custom_call" | custom-call | tf_op jit(solution)/shard_map/halo/pallas_call | solution.py:365
  17.8 7.9 %step.1 = (f32[3,512,512]{2,1,0:T(8,128)}, f32[2,512,128]{2,1,0:T(8,128)}) custom-call(s32[2,2]{1,0:T(2,128)} %offsets.1, f32[2,512,512]{2,1,0:T(8,128)} %halo.1.pad, f32[2,256,256]{2,1,0:T(8,128)} %probe.1, bf16[2,256,256]{2,1,0:T(8,128)(2,1)} %amplitudes.1, bf16[512,512]{1,0:T(8,128)(2,1)} %constant.8.clone.table_a, bf16[512,512]{1,0:T(8,128)(2,1)} %constant.9.clone.table_b), custom_call_target="tpu_custom_call" | custom-call | tf_op jit(solution)/shard_map/step/pallas_call | solution.py:376
  25.7 0.0 copy-start
  25.7 0.0 copy-start.1
  25.7 27.7 %reduce.1 = (f32[2,2,3,64,256]{4,3,2,1,0:T(8,128)}, f32[2,8,64,128]{3,2,1,0:T(8,128)}) custom-call(f32[3,4,2,64,512]{4,3,2,1,0:T(8,128)} %bitcast.17, f32[2,8,64,128]{3,2,1,0:T(8,128)} %bitcast.20), custom_call_target="tpu_custom_call" | custom-call | tf_op jit(solution)/shard_map/reduce/pallas_call | solution.py:390
  53.4 1.1 %broadcast_multiply_fusion = f32[2,8,64,128]{3,2,1,0:T(8,128)S(1)} fusion(f32[2,8,64,128]{3,2,1,0:T(8,128)} %get-tuple-element.9), kind=kLoop, calls=%fused_computation.3 | loop fusion | flops 131072 | bytes 1048576 | tf_op jit(solution)/shard_map/mul | solution.py:422
  54.5 1.0 %add_bitcast_fusion = f32[2,2,64,256]{3,2,0,1:T(8,128)S(1)} fusion(f32[2,2,3,64,256]{4,3,2,1,0:T(8,128)} %get-tuple-element.8), kind=kLoop, calls=%fused_computation.4 | loop fusion | flops 65536 | bytes 524288 | tf_op jit(solution)/shard_map/add | solution.py:419
  55.5 1.1 %slice.6 = f32[2,2,2,64,256]{4,3,2,1,0:T(8,128)S(1)} slice(f32[2,2,3,64,256]{4,3,2,1,0:T(8,128)} %get-tuple-element.8), slice={[0:2], [0:2], [0:2], [0:64], [0:256]} | slice | bytes 1048576 | tf_op jit(solution)/shard_map/slice | solution.py:417
  56.6 0.0 copy-done
  56.6 0.0 copy-done.1
  56.6 1.1 %bitcast_add_fusion = (f32[2,256,256]{2,1,0:T(8,128)}, f32[2,256,256]{2,1,0:T(8,128)}) fusion(f32[2,256,256]{2,1,0:T(8,128)S(1)} %copy-done, f32[2,2,32,8,128]{4,3,2,1,0:T(8,128)S(1)} %bitcast.18, f32[2,256,256]{2,1,0:T(8,128)S(1)} %copy-done.1, f32[256,256]{1,0:T(8,128)S(1)} %bitcast.19, f32[2,2,2,64,256]{4,3,2,1,0:T(8,128)S(1)} %slice.6), kind=kLoop, calls=%fused_computation | loop fusion | flops 393216 | bytes 3407872 | tf_op jit(solution)/shard_map/add | solution.py:422
  (1 shorter events, 0.0 us)
Async XLA Ops:
  25.7 30.9 %copy-start = (f32[2,256,256]{2,1,0:T(8,128)S(1)}, f32[2,256,256]{2,1,0:T(8,128)}, u32[]{:S(2)}) copy-start(f32[2,256,256]{2,1,0:T(8,128)} %probe.1) | copy-start | bytes 1572868
  25.7 30.9 %copy-start.1 = (f32[2,256,256]{2,1,0:T(8,128)S(1)}, f32[2,256,256]{2,1,0:T(8,128)}, u32[]{:S(2)}) copy-start(f32[2,256,256]{2,1,0:T(8,128)} %spec.1) | copy-start | bytes 1572868

commit v2 on v0

v2 whole, which is shorter than its diff:
```python
import functools
import math

import jax
import jax.numpy as jnp
import numpy as np
from jax import lax
from jax.experimental import pallas as pl
from jax.experimental.pallas import tpu as pltpu
from jax.sharding import PartitionSpec as P

MESH = pl.DeviceIdType.MESH
VMEM = pltpu.VMEM


def remote(src, dst, send, recv, where):
    return pltpu.make_async_remote_copy(
        src_ref=src, dst_ref=dst, send_sem=send, recv_sem=recv, device_id=where, device_id_type=MESH
    )


def greet(conditions_devices):
    barrier = pltpu.get_barrier_semaphore()
    for present, where in conditions_devices:
        if present is True:
            pl.semaphore_signal(barrier, inc=1, device_id=where, device_id_type=MESH)
        else:

            @pl.when(present)
            def _(where=where):
                pl.semaphore_signal(barrier, inc=1, device_id=where, device_id_type=MESH)

    fixed = sum(1 for present, _ in conditions_devices if present is True)
    peers = [present.astype(jnp.int32) for present, _ in conditions_devices if present is not True]
    pl.semaphore_wait(barrier, sum(peers, fixed))


class Side:
    def __init__(self, axis, count, step):
        me = lax.axis_index(axis)
        self.has = me > 0 if step < 0 else me < count - 1
        self.where = {axis: me + step}


class Role:
    def __init__(self, q, nx, ny):
        along_x = ("scanx", nx, Side("scanx", nx, -1), Side("scanx", nx, 1))
        along_y = ("scany", ny, Side("scany", ny, -1), Side("scany", ny, 1))
        one, two = (along_y, along_x) if q == 0 else (along_x, along_y)
        self.q, self.o, self.rows_first = q, 1 - q, q == 1
        self.axis1, self.n1, self.sides1 = one[0], one[1], one[2:]
        self.axis2, self.n2, self.sides2 = two[0], two[1], two[2:]
        self.me1, self.me2 = lax.axis_index(self.axis1), lax.axis_index(self.axis2)


def when(*conditions):
    return pl.when(functools.reduce(jnp.logical_and, conditions))


def dot(a, b):
    return jnp.dot(a, b, preferred_element_type=jnp.float32)


class Halo:
    def __init__(self, role, spec, pad, send, recv, partner):
        self.r, self.spec, self.pad, self.partner = role, spec, pad, partner
        self.send, self.recv = send, recv
        tile = spec.shape[1]
        half = (pad.shape[1] - tile) // 2
        self.own = pl.ds(half, tile)
        self.margins = (pl.ds(0, half), pl.ds(half + tile, half))
        self.edges = (pl.ds(0, half), pl.ds(tile - half, half))
        self.pad_edges = (pl.ds(half, half), pl.ds(tile, half))
        self.whole = pl.ds(0, tile)

    def at(self, one, two):
        return (self.r.q, one, two) if self.r.rows_first else (self.r.q, two, one)

    def copy(self, src, dst, i, where):
        return remote(src, dst, self.send.at[i], self.recv.at[i], where)

    def strip1(self, m):
        return self.copy(
            self.spec.at[self.at(self.edges[1 - m], self.whole)],
            self.pad.at[self.at(self.margins[m], self.own)],
            m,
            self.r.sides1[1 - m].where,
        )

    def strip2(self, m):
        return self.copy(
            self.spec.at[self.at(self.whole, self.edges[1 - m])],
            self.pad.at[self.at(self.own, self.margins[m])],
            2 + m,
            self.r.sides2[1 - m].where,
        )

    def corner(self, m1, m2):
        return self.copy(
            self.pad.at[self.at(self.margins[m1], self.pad_edges[1 - m2])],
            self.pad.at[self.at(self.margins[m1], self.margins[m2])],
            4 + 2 * m1 + m2,
            self.r.sides2[1 - m2].where,
        )

    def share(self, i, one, two):
        ref = self.pad.at[self.at(one, two)]
        return self.copy(ref, ref, 8 + i, self.partner)

    def share1(self, m):
        return self.share(m, self.margins[m], self.own)

    def share2(self, m):
        return self.share(2 + m, self.own, self.margins[m])

    def share_corner(self, m1, m2):
        return self.share(4 + 2 * m1 + m2, self.margins[m1], self.margins[m2])

    def begin(self):
        for m in range(2):
            when(self.r.sides1[1 - m].has)(self.strip1(m).start)
        for m in range(2):
            when(self.r.sides2[1 - m].has)(self.strip2(m).start)

    def relay(self):
        r = self.r
        for m1 in range(2):

            @when(r.sides1[m1].has)
            def _():
                self.strip1(m1).wait_recv()
                for m2 in range(2):
                    when(r.sides2[1 - m2].has)(self.corner(m1, m2).start)
                self.share1(m1).start()

        for m in range(2):

            @when(r.sides2[m].has)
            def _():
                self.strip2(m).wait_recv()
                self.share2(m).start()

        for m1 in range(2):
            for m2 in range(2):

                @when(r.sides1[m1].has, r.sides2[m2].has)
                def _():
                    self.corner(m1, m2).wait_recv()
                    self.share_corner(m1, m2).start()

    def arrive(self):
        r = self.r
        for m in range(2):
            when(r.sides1[m].has)(self.share1(m).wait_recv)
            when(r.sides2[m].has)(self.share2(m).wait_recv)
        for m1 in range(2):
            for m2 in range(2):
                when(r.sides1[m1].has, r.sides2[m2].has)(self.share_corner(m1, m2).wait_recv)

    def finish(self):
        r = self.r
        for m in range(2):
            when(r.sides1[1 - m].has)(self.strip1(m).wait_send)
            when(r.sides2[1 - m].has)(self.strip2(m).wait_send)
            when(r.sides1[m].has)(self.share1(m).wait_send)
            when(r.sides2[m].has)(self.share2(m).wait_send)
        for m1 in range(2):
            for m2 in range(2):
                when(r.sides1[m1].has, r.sides2[1 - m2].has)(self.corner(m1, m2).wait_send)
                when(r.sides1[m1].has, r.sides2[m2].has)(self.share_corner(m1, m2).wait_send)


class Fold:
    def __init__(self, role, mine, theirs, pair, acc, rims, core, send, recv, partner):
        self.r, self.mine, self.theirs, self.pair, self.acc = role, mine, theirs, pair, acc
        self.xr1, self.xr2, self.zr1, self.zr2 = rims
        self.core, self.send, self.recv, self.partner = core, send, recv, partner
        w = acc.shape[-1]
        self.w, self.q4 = w, w // 4

    def pieces(self, rows):
        q4, w = self.q4, self.w
        if rows:
            return [(pl.ds(0, 1),), (pl.ds(3, 1),), (pl.ds(1, 2),)]
        lead = (slice(None),) * 3
        return [lead + (pl.ds(0, q4),), lead + (pl.ds(3 * q4, q4),), lead + (pl.ds(q4, 2 * q4),)]

    def pair_copy(self, i, rows):
        at = self.pieces(rows)[i]
        return remote(self.theirs.at[at], self.pair.at[at], self.send.at[i], self.recv.at[i], self.partner)

    def begin(self):
        for i in range(3):
            self.pair_copy(i, not self.r.rows_first).start()

    def add(self, i):
        self.pair_copy(i, self.r.rows_first).wait_recv()
        at = self.pieces(self.r.rows_first)[i]
        self.acc[at] = self.mine[at] + self.pair[at]

    def rim_copy(self, stage, m):
        r, q4, w = self.r, self.q4, self.w
        rows = r.rows_first == (stage == 0)
        k = 1 - m
        if rows:
            cols = pl.ds(0, w) if stage == 0 else pl.ds(q4, 2 * q4)
            src = self.acc.at[3 * k, :, :, cols]
            rim = self.zr1 if stage == 0 else self.zr2
        else:
            groups = pl.ds(0, 4) if stage == 0 else pl.ds(1, 2)
            src = self.acc.at[groups, :, :, pl.ds(3 * k * q4, q4)]
            rim = self.xr1 if stage == 0 else self.xr2
        sides = r.sides1 if stage == 0 else r.sides2
        i = 3 + 2 * stage + m
        return remote(src, rim.at[m], self.send.at[i], self.recv.at[i], sides[k].where)

    def send_rims(self, stage):
        sides = self.r.sides1 if stage == 0 else self.r.sides2
        for m in range(2):
            when(sides[1 - m].has)(self.rim_copy(stage, m).start)

    def fold(self, stage):
        r, q4, w, acc = self.r, self.q4, self.w, self.acc
        rows = r.rows_first == (stage == 0)
        sides = r.sides1 if stage == 0 else r.sides2
        for m in range(2):

            @when(sides[m].has)
            def _():
                self.rim_copy(stage, m).wait_recv()
                if rows:
                    cols = pl.ds(0, w) if stage == 0 else pl.ds(q4, 2 * q4)
                    rim = self.zr1 if stage == 0 else self.zr2
                    acc[1 + m, :, :, cols] = acc[1 + m, :, :, cols] + rim[m]
                else:
                    groups = pl.ds(0, 4) if stage == 0 else pl.ds(1, 2)
                    cols = pl.ds((1 + m) * q4, q4)
                    rim = self.xr1 if stage == 0 else self.xr2
                    acc[groups, :, :, cols] = acc[groups, :, :, cols] + rim[m]

    def share_copy(self, q):
        return remote(self.core.at[q], self.core.at[q], self.send.at[7], self.recv.at[7], self.partner)

    def share(self):
        q4 = self.q4
        self.core[self.r.q] = self.acc[1:3, :, :, q4 : 3 * q4]
        self.share_copy(self.r.q).start()

    def arrive(self):
        self.share_copy(self.r.o).wait_recv()

    def finish(self):
        r = self.r
        for i in range(3):
            self.pair_copy(i, not r.rows_first).wait_send()
        for m in range(2):
            when(r.sides1[1 - m].has)(self.rim_copy(0, m).wait_send)
            when(r.sides2[1 - m].has)(self.rim_copy(1, m).wait_send)
        self.share_copy(r.q).wait_send()


class ProbeSum:
    def __init__(self, role, mine, theirs, ppair, pacc, p1, pr1, pr2, total, send, recv, partner):
        self.r, self.mine, self.theirs = role, mine, theirs
        self.ppair, self.pacc, self.p1 = ppair, pacc, p1
        self.pr1, self.pr2, self.total = pr1, pr2, total
        self.send, self.recv, self.partner = send, recv, partner

    def copy(self, src, dst, stage, d, where):
        return remote(src, dst, self.send.at[stage, d], self.recv.at[stage, d], where)

    def pair_copy(self):
        return self.copy(self.theirs, self.ppair, 0, 0, self.partner)

    def begin(self):
        self.pair_copy().start()

    def scatter1(self):
        r = self.r
        out = []
        for d in range(1, r.n1):
            j = lax.rem(r.me1 + d, r.n1)
            src = self.pacc.at[pl.ds(j * r.n2, r.n2)]
            out.append(self.copy(src, self.pr1.at[pl.ds(d * r.n2, r.n2)], 1, d, {r.axis1: j}))
        return out

    def scatter2(self):
        r = self.r
        out = []
        for d in range(1, r.n2):
            j = lax.rem(r.me2 + d, r.n2)
            out.append(self.copy(self.p1.at[pl.ds(j, 1)], self.pr2.at[pl.ds(d, 1)], 2, d, {r.axis2: j}))
        return out

    def gather2(self, back):
        r = self.r
        out = []
        for d in range(1, r.n2):
            j = lax.rem(r.me2 + d, r.n2)
            origin = lax.rem(r.me2 - d + r.n2, r.n2) if back else r.me2
            ref = self.total.at[r.q, pl.ds(r.me1 * r.n2 + origin, 1)]
            out.append(self.copy(ref, ref, 3, d, {r.axis2: j}))
        return out

    def gather1(self, back):
        r = self.r
        out = []
        for d in range(1, r.n1):
            j = lax.rem(r.me1 + d, r.n1)
            origin = lax.rem(r.me1 - d + r.n1, r.n1) if back else r.me1
            ref = self.total.at[r.q, pl.ds(origin * r.n2, r.n2)]
            out.append(self.copy(ref, ref, 4, d, {r.axis1: j}))
        return out

    def share_copy(self, d, sender):
        r = self.r
        origin = lax.rem(r.me1 - d + r.n1, r.n1)
        ref = self.total.at[r.q, pl.ds(origin * r.n2, r.n2)]
        return self.copy(ref, ref, 5, d, self.partner)

    def step1(self):
        self.pair_copy().wait_recv()
        self.pacc[...] = self.mine[...] + self.ppair[...]
        for c in self.scatter1():
            c.start()

    def step2(self):
        r = self.r
        mine = self.pacc[pl.ds(r.me1 * r.n2, r.n2)]
        for d, c in enumerate(self.scatter1(), 1):
            c.wait_recv()
            mine = mine + self.pr1[d * r.n2 : (d + 1) * r.n2]
        self.p1[0 : r.n2] = mine
        for c in self.scatter2():
            c.start()

    def step3(self):
        r = self.r
        one = self.p1[pl.ds(r.me2, 1)]
        for d, c in enumerate(self.scatter2(), 1):
            c.wait_recv()
            one = one + self.pr2[d : d + 1]
        self.total[r.q, pl.ds(r.me1 * r.n2 + r.me2, 1)] = one
        for c in self.gather2(0):
            c.start()

    def step4(self):
        for c in self.gather2(1):
            c.wait_recv()
        for c in self.gather1(0):
            c.start()
        self.share_copy(0, True).start()

    def step5(self):
        for d, c in enumerate(self.gather1(1), 1):
            c.wait_recv()
            self.share_copy(d, True).start()

    def arrive(self):
        for d in range(self.r.n1):
            self.share_copy(d, False).wait_recv()

    def finish(self):
        self.pair_copy().wait_send()
        for c in self.scatter1() + self.scatter2() + self.gather2(0) + self.gather1(0):
            c.wait_send()
        for d in range(self.r.n1):
            self.share_copy(d, True).wait_send()


def line_greet(nx, ny, partner):
    mx, my = lax.axis_index("scanx"), lax.axis_index("scany")
    greet(
        [(True, partner)]
        + [(True, {"scanx": lax.rem(mx + d, nx)}) for d in range(1, nx)]
        + [(True, {"scany": lax.rem(my + d, ny)}) for d in range(1, ny)]
    )


def each(step):
    p = lax.axis_index("pos")
    for q in range(2):
        pl.when(p == q)(functools.partial(step, q))


def halo_kernel(nx, ny, spec, pad, send, recv, local):
    tile = spec.shape[1]
    half = (pad.shape[1] - tile) // 2
    own = pl.ds(half, tile)
    partner = {"pos": 1 - lax.axis_index("pos")}
    centre = pltpu.make_async_copy(spec, pad.at[:, own, own], local.at[0])
    centre.start()
    roles = [Role(q, nx, ny) for q in range(2)]
    sides = roles[1].sides1 + roles[0].sides1
    greet([(True, partner)] + [(side.has, side.where) for side in sides])
    halos = [Halo(r, spec, pad, send, recv, partner) for r in roles]
    each(lambda q: halos[q].begin())
    for i, at in enumerate(
        (
            (slice(None), pl.ds(0, half)),
            (slice(None), pl.ds(half + tile, half)),
            (slice(None), slice(None), pl.ds(0, half)),
            (slice(None), slice(None), pl.ds(half + tile, half)),
        )
    ):

        @pl.when(jnp.logical_not(sides[i].has))
        def _(at=at):
            pad[at] = jnp.zeros(pad.at[at].shape, pad.dtype)

    def rest(q):
        halos[q].relay()
        halos[1 - q].arrive()
        halos[q].finish()

    each(rest)
    centre.wait()


def step_kernel(offsets, pad, probe, amplitudes, table_a, table_b, grad_out, prob, grad, local):
    m = probe.shape[1]
    tall, span = m + 8, m + 128
    pr, pi = probe[0], probe[1]
    grad[...] = jnp.zeros(grad.shape, grad.dtype)
    blank_rows = jnp.zeros((tall - m, m), jnp.float32)
    blank_cols = jnp.zeros((tall, span - m), jnp.float32)
    bf = jnp.bfloat16
    positions = amplitudes.shape[0]

    def place_at(j):
        row, col = offsets[j, 0], offsets[j, 1]
        row_in, col_in = lax.rem(row, 8), lax.rem(col, 128)
        rows = pl.ds(pl.multiple_of(row - row_in, 8), tall)
        cols = pl.ds(pl.multiple_of(col - col_in, 128), span)
        return row_in, col_in, rows, cols

    def place(j, k, term):
        row_in, col_in, rows, cols = place_at(j)
        moved = pltpu.roll(jnp.concatenate([term, blank_rows], 0), row_in, 0)
        moved = pltpu.roll(jnp.concatenate([moved, blank_cols], 1), col_in, 1)
        grad[k, rows, cols] = grad[k, rows, cols] + moved

    outs = [pltpu.make_async_copy(grad.at[k], grad_out.at[k], local.at[k]) for k in range(3)]
    power = pr * pr + pi * pi
    for j in range(positions):
        place(j, 2, power)
    outs[2].start()
    sum_r = sum_i = None
    for j in range(positions):
        row_in, col_in, rows, cols = place_at(j)

        def window(k):
            block = pad[k, rows, cols]
            block = pltpu.roll(block, lax.rem(span - col_in, span), 1)[:, :m]
            return pltpu.roll(block, lax.rem(tall - row_in, tall), 0)[:m]

        ar, ai = window(0), window(1)
        er = pr * ar - pi * ai
        ei = pr * ai + pi * ar
        left = dot(table_a[...], jnp.concatenate([er.astype(bf), ei.astype(bf)], 0)).astype(bf)
        far = dot(jnp.concatenate([left[:m], left[m:]], 1), table_b[...])
        fr, fi = far[:, :m], far[:, m:]
        ratio = amplitudes[j].astype(jnp.float32) / jnp.maximum(jnp.sqrt(fr * fr + fi * fi), 0.2)
        projected = jnp.concatenate([(fr * ratio).astype(bf), (fi * ratio).astype(bf)], 0)
        back_half = dot(table_b[...], projected).astype(bf)
        back = dot(jnp.concatenate([back_half[:m], back_half[m:]], 1), table_a[...])
        dr = back[:, :m] - er
        di = back[:, m:] - ei
        tr = ar * dr + ai * di
        ti = ar * di - ai * dr
        sum_r = tr if sum_r is None else sum_r + tr
        sum_i = ti if sum_i is None else sum_i + ti
        place(j, 0, pr * dr + pi * di)
        if j == positions - 1:
            outs[0].start()
        place(j, 1, pr * di - pi * dr)
    outs[1].start()
    n, s, lanes = prob.shape[1:]
    for k, value in enumerate((sum_r, sum_i)):
        for c in range(n):
            r0, l0 = c * s % m, c * s // m * lanes
            prob[k, c] = value[r0 : r0 + s, l0 : l0 + lanes]
    for c in outs:
        c.wait()


def reduce_kernel(nx, ny, step_size, *refs):
    grad, prob, spec_in, probe_in, new_spec, new_probe = refs[:6]
    spec, probe, mine, imine, pmine, total = refs[6:12]
    (pair, acc, xr1, xr2, zr1, zr2, core, ipair, iacc, ixr1, ixr2, izr1, izr2, icore) = refs[12:26]
    (ppair, pacc, p1, pr1, pr2) = refs[26:31]
    (gsend, grecv, isend, irecv, psend, precv, local) = refs[31:]
    m = probe.shape[1]
    h = acc.shape[2]
    p = lax.axis_index("pos")
    partner = {"pos": 1 - p}
    loads = [
        pltpu.make_async_copy(src, dst, local.at[i])
        for i, (src, dst) in enumerate(
            (
                (prob.at[p], pmine),
                (grad.at[p], mine),
                (grad.at[2, :, pl.ds(p, 1)], imine),
                (spec_in, spec),
                (probe_in, probe),
            )
        )
    ]
    for c in loads:
        c.start()
    line_greet(nx, ny, partner)
    roles = [Role(q, nx, ny) for q in range(2)]
    folds = [
        Fold(r, mine, grad.at[r.o], pair, acc, (xr1, xr2, zr1, zr2), core, gsend, grecv, partner)
        for r in roles
    ]
    lights = [
        Fold(
            r,
            imine,
            grad.at[2, :, pl.ds(r.o, 1)],
            ipair,
            iacc,
            (ixr1, ixr2, izr1, izr2),
            icore,
            isend,
            irecv,
            partner,
        )
        for r in roles
    ]
    probes = [
        ProbeSum(r, pmine, prob.at[r.o], ppair, pacc, p1, pr1, pr2, total, psend, precv, partner)
        for r in roles
    ]

    def objects(q):
        probe_sum, fold, light = probes[q], folds[q], lights[q]
        probe_sum.begin()
        fold.begin()
        light.begin()
        loads[0].wait()
        probe_sum.step1()
        loads[1].wait()
        fold.add(0)
        fold.add(1)
        fold.send_rims(0)
        loads[2].wait()
        light.add(0)
        light.add(1)
        light.send_rims(0)
        fold.add(2)
        light.add(2)
        probe_sum.step2()
        fold.fold(0)
        fold.send_rims(1)
        light.fold(0)
        light.send_rims(1)
        probe_sum.step3()
        fold.fold(1)
        fold.share()
        light.fold(1)
        light.share()
        probe_sum.step4()
        light.arrive()
        fold.arrive()

    each(objects)
    loads[3].wait()
    for k in range(2):
        for g in range(2):
            for b in range(2):
                rows = slice((2 * g + b) * h, (2 * g + b + 1) * h)
                new_spec[k, rows] = spec[k, rows] + core[k, g, b] / (icore[b, g, 0] + 1.0)

    def closing(q):
        probes[q].step5()
        probes[1 - q].arrive()
        lights[q].finish()
        folds[q].finish()
        probes[q].finish()

    each(closing)
    loads[4].wait()
    n, s, lanes = prob.shape[1:]
    for k in range(2):
        for c in range(n):
            rows = slice(c * s % m, c * s % m + s)
            cols = slice(c * s // m * lanes, c * s // m * lanes + lanes)
            new_probe[k, rows, cols] = probe[k, rows, cols] + total[k, c] * step_size


def tables(length):
    index = np.arange(length)
    angle = ((index[:, None] * index[None, :]) % length).astype(np.float32) * np.float32(2.0 * math.pi / length)
    scale = np.float32(1.0 / math.sqrt(length))
    c = np.cos(angle) * scale
    s = np.sin(angle) * scale
    a = np.block([[c, s], [-s, c]]).astype(jnp.bfloat16)
    b = np.block([[c, -s], [s, c]]).astype(jnp.bfloat16)
    return a, b


def shards(nx, ny, consts, specimen, probe_wave, amplitudes, offsets):
    m = probe_wave.shape[1]
    tile = specimen.shape[1]
    wide = tile + m
    f32 = jnp.float32
    vm = pl.BlockSpec(memory_space=VMEM)
    sm = pl.BlockSpec(memory_space=pltpu.SMEM)
    anywhere = pl.BlockSpec(memory_space=pl.ANY)
    dma = pltpu.SemaphoreType.DMA
    lanes = 128
    n = nx * ny
    s = m * m // lanes // n
    h = wide // 8
    most = max(nx, ny)
    positions = offsets.shape[0]
    pad = pl.pallas_call(
        functools.partial(halo_kernel, nx, ny),
        out_shape=jax.ShapeDtypeStruct((2, wide, wide), f32),
        in_specs=[anywhere],
        out_specs=vm,
        scratch_shapes=[dma((16,)), dma((16,)), dma((1,))],
        compiler_params=pltpu.CompilerParams(collective_id=0, has_side_effects=True),
        name="halo",
    )(specimen)
    grad, prob = pl.pallas_call(
        step_kernel,
        out_shape=[
            jax.ShapeDtypeStruct((3, wide, wide), f32),
            jax.ShapeDtypeStruct((2, n, s, lanes), f32),
        ],
        in_specs=[sm] + [vm] * 5,
        out_specs=[anywhere, vm],
        scratch_shapes=[VMEM((3, wide, wide), f32), dma((3,))],
        name="step",
    )(offsets, pad, probe_wave, amplitudes, consts[0], consts[1])

    def field(size):
        return [
            VMEM((4, size, h, wide), f32),
            VMEM((4, size, h, wide), f32),
            VMEM((2, 4, size, h, wide // 4), f32),
            VMEM((2, 2, size, h, wide // 4), f32),
            VMEM((2, size, h, wide), f32),
            VMEM((2, size, h, wide // 2), f32),
            VMEM((2, 2, size, h, wide // 2), f32),
        ]

    step_size = 1.0 / math.sqrt(positions * n * 2)
    return pl.pallas_call(
        functools.partial(reduce_kernel, nx, ny, step_size),
        out_shape=[
            jax.ShapeDtypeStruct(specimen.shape, f32),
            jax.ShapeDtypeStruct(probe_wave.shape, f32),
        ],
        in_specs=[anywhere] * 4,
        out_specs=[vm, vm],
        scratch_shapes=[
            VMEM(specimen.shape, f32),
            VMEM(probe_wave.shape, f32),
            VMEM((4, 2, h, wide), f32),
            VMEM((4, 1, h, wide), f32),
            VMEM((n, s, lanes), f32),
            VMEM((2, n, s, lanes), f32),
            *field(2),
            *field(1),
            VMEM((n, s, lanes), f32),
            VMEM((n, s, lanes), f32),
            VMEM((most, s, lanes), f32),
            VMEM((n, s, lanes), f32),
            VMEM((most, s, lanes), f32),
            dma((8,)),
            dma((8,)),
            dma((8,)),
            dma((8,)),
            dma((6, most)),
            dma((6, most)),
            dma((5,)),
        ],
        compiler_params=pltpu.CompilerParams(collective_id=1, has_side_effects=True),
        name="reduce",
    )(grad.reshape(3, 4, 2, h, wide), prob, specimen, probe_wave)


def solution(mesh):
    nx, ny = mesh.shape["scanx"], mesh.shape["scany"]

    def run(specimen, probe_wave, amplitudes, offsets):
        consts = tables(probe_wave.shape[2])
        return jax.shard_map(
            lambda *args: shards(nx, ny, [jnp.asarray(t) for t in consts], *args),
            mesh=mesh,
            in_specs=(
                P(None, ("groups", "scanx"), "scany"),
                P(None, "groups", None),
                P(("groups", "scanx", "scany", "pos"), None, None),
                P(("groups", "scanx", "scany", "pos"), None),
            ),
            out_specs=(P(None, ("groups", "scanx"), "scany"), P(None, "groups", None)),
            check_vma=False,
        )(specimen, probe_wave, amplitudes, offsets)

    return run
```

time: 251 us -> 51.2 us (0.20)
  waiting for transfers between devices: 143 us -> 0 us
  Pallas kernels: 0 us -> 46.6 us
  other arithmetic: 29.9 us -> 0 us
  local copies, waits for them, and re-layouts: 27.4 us -> 3.74 us
  starting transfers between devices: 19.8 us -> 0 us
  between operations: 14.2 us -> 0.65 us
  matrix products: 7.75 us -> 0 us
  loops' own time: 7.59 us -> 0 us
    psum x2 -> x0, waiting for transfers between devices: 101 us -> none  [the longest x1 81.5 us: shards(): total_grad = lax.psum(probe_grad, ('scanx', 'scany', 'pos'))]
    pallas_call x0 -> x3, Pallas kernels: none -> 46.6 us  [the longest x1 24 us: shards(): pl.pallas_call(functools.partial(reduce_kernel, nx, ny, step_size), out_s...]
    ppermute x8 -> x0, waiting for transfers between devices: 41.7 us -> none  [the longest x4 28.4 us: padded_2(): lax.ppermute(lax.slice_in_dim(block, block.shape[dim] - width, None, axis...]
    ppermute x8 -> x0, starting transfers between devices: 19.8 us -> none  [the longest x4 14.6 us: padded_2(): lax.ppermute(lax.slice_in_dim(block, block.shape[dim] - width, None, axis...]
    dynamic_update_slice x2 -> x0, local copies, waits for them, and re-layouts: 18 us -> none  [visit_position(): lax.dynamic_update_slice(object_grad, current + object_term, (zero_index,...]
    add x13 -> x0, other arithmetic: 17 us -> none  [the longest x2 3.32 us: visit_position(): current + object_term]
    dot_general x4 -> x0, matrix products: 7.75 us -> none  [the longest x2 3.96 us: project_exit(): jnp.einsum('bkv,bval->akl', back_half, inverse_right, preferred_element_t...]
    another operation x1 -> x0, loops' own time: 7.59 us -> none  [shards(): lax.scan(visit_position, (start_grad, start_probe), (amplitudes, offsets))]
  transfers between devices with their start and end apart: 10 -> 0, of which waited for: 9 -> 0; matrix products, arithmetic and copies ran while one was open for 3% -> 0% of each run, Pallas kernels for 0% -> 0%
where the time goes in v2:
time: 51.2 us; the launch traced here: 51 us
  Pallas kernels  46.6 us (91%)
  local copies, waits for them, and re-layouts  3.74 us (7%)
  between operations  0.65 us (1%)
    pallas_call x1, Pallas kernels, shards(): pl.pallas_call(functools.partial(reduce_kernel, nx, ny, step_size), out_s...  24 us
    pallas_call x1, Pallas kernels, shards(): pl.pallas_call(functools.partial(halo_kernel, nx, ny), out_shape=jax.Shap...  14.4 us
    pallas_call x1, Pallas kernels, shards(): pl.pallas_call(step_kernel, out_shape=[jax.ShapeDtypeStruct((3, wide, wid...  8.2 us
    unnamed x2, local copies, waits for them, and re-layouts  3.74 us

profile of v2, /device:TPU:0, one launch (start us, length us, event | category | flops | bytes accessed | tf_op | source)
XLA Modules:
  0.0 51.0 jit_solution(5784913940193526308)
XLA Ops:
  0.6 14.4 %halo.1.pad = f32[2,512,512]{2,1,0:T(8,128)} custom-call(f32[2,256,256]{2,1,0:T(8,128)} %refs_2_.1), custom_call_target="tpu_custom_call" | custom-call | tf_op jit(solution)/shard_map/halo/pallas_call | solution.py:619
  15.1 8.2 %step.1 = (f32[3,512,512]{2,1,0:T(8,128)}, f32[2,8,64,128]{3,2,1,0:T(8,128)}) custom-call(s32[2,2]{1,0:T(2,128)} %offsets.1, f32[2,512,512]{2,1,0:T(8,128)} %halo.1.pad, f32[2,256,256]{2,1,0:T(8,128)} %refs_3_.1, bf16[2,256,256]{2,1,0:T(8,128)(2,1)} %amplitudes.1, bf16[512,512]{1,0:T(8,128)(2,1)} %constant.4.clone.table_a, ...), custom_call_target="tpu_custom_call" | custom-call | tf_op jit(solution)/shard_map/step/pallas_call | solution.py:628
  23.3 24.0 %reduce.1 = (f32[2,256,256]{2,1,0:T(8,128)}, f32[2,256,256]{2,1,0:T(8,128)}) custom-call(f32[3,4,2,64,512]{4,3,2,1,0:T(8,128)} %bitcast.1, f32[2,8,64,128]{3,2,1,0:T(8,128)} %get-tuple-element.5.refs_1_, f32[2,256,256]{2,1,0:T(8,128)} %refs_2_.1, f32[2,256,256]{2,1,0:T(8,128)} %refs_3_.1), custom_call_target="tpu_custom_call" | custom-call | tf_op jit(solution)/shard_map/reduce/pallas_call | solution.py:652
  47.2 1.9 %copy.10 = f32[2,256,256]{2,1,0:T(8,128)} copy(f32[2,256,256]{2,1,0:T(8,128)} %get-tuple-element.8) | data formatting | bytes 1048576
  49.1 1.9 %copy.11 = f32[2,256,256]{2,1,0:T(8,128)} copy(f32[2,256,256]{2,1,0:T(8,128)} %get-tuple-element.9) | data formatting | bytes 1048576

commit v3 on v2

--- a/solution.py
+++ b/solution.py
@@ -383,13 +383,18 @@
         pl.when(p == q)(functools.partial(step, q))
 
 
-def halo_kernel(nx, ny, spec, pad, send, recv, local):
+def halo_kernel(nx, ny, spec, *refs):
+    loaded, pad, kept = refs[:5], refs[5], refs[6:11]
+    send, recv, local = refs[11:]
     tile = spec.shape[1]
     half = (pad.shape[1] - tile) // 2
     own = pl.ds(half, tile)
     partner = {"pos": 1 - lax.axis_index("pos")}
-    centre = pltpu.make_async_copy(spec, pad.at[:, own, own], local.at[0])
-    centre.start()
+    loads = [pltpu.make_async_copy(spec, pad.at[:, own, own], local.at[0])]
+    for i, (src, dst) in enumerate(zip(loaded, kept), 1):
+        loads.append(pltpu.make_async_copy(src, dst, local.at[i]))
+    for c in loads:
+        c.start()
     roles = [Role(q, nx, ny) for q in range(2)]
     sides = roles[1].sides1 + roles[0].sides1
     greet([(True, partner)] + [(side.has, side.where) for side in sides])
@@ -414,10 +419,11 @@
         halos[q].finish()
 
     each(rest)
-    centre.wait()
-
-
-def step_kernel(offsets, pad, probe, amplitudes, table_a, table_b, grad_out, prob, grad, local):
+    for c in loads:
+        c.wait()
+
+
+def step_kernel(offsets, pad, probe, amplitudes, table_a, table_b, grad, prob):
     m = probe.shape[1]
     tall, span = m + 8, m + 128
     pr, pi = probe[0], probe[1]
@@ -440,11 +446,9 @@
         moved = pltpu.roll(jnp.concatenate([moved, blank_cols], 1), col_in, 1)
         grad[k, rows, cols] = grad[k, rows, cols] + moved
 
-    outs = [pltpu.make_async_copy(grad.at[k], grad_out.at[k], local.at[k]) for k in range(3)]
     power = pr * pr + pi * pi
     for j in range(positions):
         place(j, 2, power)
-    outs[2].start()
     sum_r = sum_i = None
     for j in range(positions):
         row_in, col_in, rows, cols = place_at(j)
@@ -471,53 +475,31 @@
         sum_r = tr if sum_r is None else sum_r + tr
         sum_i = ti if sum_i is None else sum_i + ti
         place(j, 0, pr * dr + pi * di)
-        if j == positions - 1:
-            outs[0].start()
         place(j, 1, pr * di - pi * dr)
-    outs[1].start()
     n, s, lanes = prob.shape[1:]
     for k, value in enumerate((sum_r, sum_i)):
         for c in range(n):
             r0, l0 = c * s % m, c * s // m * lanes
             prob[k, c] = value[r0 : r0 + s, l0 : l0 + lanes]
-    for c in outs:
-        c.wait()
-
-
-def reduce_kernel(nx, ny, step_size, *refs):
-    grad, prob, spec_in, probe_in, new_spec, new_probe = refs[:6]
-    spec, probe, mine, imine, pmine, total = refs[6:12]
-    (pair, acc, xr1, xr2, zr1, zr2, core, ipair, iacc, ixr1, ixr2, izr1, izr2, icore) = refs[12:26]
-    (ppair, pacc, p1, pr1, pr2) = refs[26:31]
-    (gsend, grecv, isend, irecv, psend, precv, local) = refs[31:]
-    m = probe.shape[1]
-    h = acc.shape[2]
+
+
+def reduce_kernel(nx, ny, *refs):
+    grad, prob, core, icore, total = refs[:5]
+    (pair, acc, xr1, xr2, zr1, zr2, ipair, iacc, ixr1, ixr2, izr1, izr2) = refs[5:17]
+    (ppair, pacc, p1, pr1, pr2) = refs[17:22]
+    (gsend, grecv, isend, irecv, psend, precv) = refs[22:]
     p = lax.axis_index("pos")
     partner = {"pos": 1 - p}
-    loads = [
-        pltpu.make_async_copy(src, dst, local.at[i])
-        for i, (src, dst) in enumerate(
-            (
-                (prob.at[p], pmine),
-                (grad.at[p], mine),
-                (grad.at[2, :, pl.ds(p, 1)], imine),
-                (spec_in, spec),
-                (probe_in, probe),
-            )
-        )
-    ]
-    for c in loads:
-        c.start()
     line_greet(nx, ny, partner)
     roles = [Role(q, nx, ny) for q in range(2)]
     folds = [
-        Fold(r, mine, grad.at[r.o], pair, acc, (xr1, xr2, zr1, zr2), core, gsend, grecv, partner)
+        Fold(r, grad.at[r.q], grad.at[r.o], pair, acc, (xr1, xr2, zr1, zr2), core, gsend, grecv, partner)
         for r in roles
     ]
     lights = [
         Fold(
             r,
-            imine,
+            grad.at[2, :, pl.ds(r.q, 1)],
             grad.at[2, :, pl.ds(r.o, 1)],
             ipair,
             iacc,
@@ -530,7 +512,7 @@
         for r in roles
     ]
     probes = [
-        ProbeSum(r, pmine, prob.at[r.o], ppair, pacc, p1, pr1, pr2, total, psend, precv, partner)
+        ProbeSum(r, prob.at[r.q], prob.at[r.o], ppair, pacc, p1, pr1, pr2, total, psend, precv, partner)
         for r in roles
     ]
 
@@ -539,13 +521,10 @@
         probe_sum.begin()
         fold.begin()
         light.begin()
-        loads[0].wait()
         probe_sum.step1()
-        loads[1].wait()
         fold.add(0)
         fold.add(1)
         fold.send_rims(0)
-        loads[2].wait()
         light.add(0)
         light.add(1)
         light.send_rims(0)
@@ -566,13 +545,6 @@
         fold.arrive()
 
     each(objects)
-    loads[3].wait()
-    for k in range(2):
-        for g in range(2):
-            for b in range(2):
-                rows = slice((2 * g + b) * h, (2 * g + b + 1) * h)
-                new_spec[k, rows] = spec[k, rows] + core[k, g, b] / (icore[b, g, 0] + 1.0)
-
     def closing(q):
         probes[q].step5()
         probes[1 - q].arrive()
@@ -581,8 +553,19 @@
         probes[q].finish()
 
     each(closing)
-    loads[4].wait()
-    n, s, lanes = prob.shape[1:]
+
+def apply_kernel(step_size, core, light, total, pad, probe, new_spec, new_probe):
+    tile = new_spec.shape[1]
+    half = (pad.shape[1] - tile) // 2
+    m = probe.shape[1]
+    h = core.shape[3]
+    for k in range(2):
+        for g in range(2):
+            for b in range(2):
+                r0 = (2 * g + b) * h
+                old = pad[k, half + r0 : half + r0 + h, half : half + tile]
+                new_spec[k, r0 : r0 + h] = old + core[k, g, b] / (light[b, g, 0] + 1.0)
+    n, s, lanes = total.shape[1:]
     for k in range(2):
         for c in range(n):
             rows = slice(c * s % m, c * s % m + s)
@@ -616,15 +599,18 @@
     h = wide // 8
     most = max(nx, ny)
     positions = offsets.shape[0]
-    pad = pl.pallas_call(
+    shaped = VMEM
+    held = (offsets, probe_wave, amplitudes, consts[0], consts[1])
+    hbm = pl.BlockSpec(memory_space=pltpu.HBM)
+    pad, *held = pl.pallas_call(
         functools.partial(halo_kernel, nx, ny),
-        out_shape=jax.ShapeDtypeStruct((2, wide, wide), f32),
-        in_specs=[anywhere],
-        out_specs=vm,
-        scratch_shapes=[dma((16,)), dma((16,)), dma((1,))],
-        compiler_params=pltpu.CompilerParams(collective_id=0, has_side_effects=True),
+        out_shape=[shaped((2, wide, wide), f32)] + [shaped(x.shape, x.dtype) for x in held],
+        in_specs=[hbm] * 6,
+        out_specs=[vm] * 6,
+        scratch_shapes=[dma((16,)), dma((16,)), dma((6,))],
+        compiler_params=pltpu.CompilerParams(vmem_limit_bytes=16 * 2**20, collective_id=0, has_side_effects=True),
         name="halo",
-    )(specimen)
+    )(*[pltpu.with_memory_space_constraint(x, pltpu.HBM) for x in (specimen, *held)])
     grad, prob = pl.pallas_call(
         step_kernel,
         out_shape=[
@@ -632,10 +618,10 @@
             jax.ShapeDtypeStruct((2, n, s, lanes), f32),
         ],
         in_specs=[sm] + [vm] * 5,
-        out_specs=[anywhere, vm],
-        scratch_shapes=[VMEM((3, wide, wide), f32), dma((3,))],
+        out_specs=[vm, vm],
+        compiler_params=pltpu.CompilerParams(vmem_limit_bytes=32 * 2**20),
         name="step",
-    )(offsets, pad, probe_wave, amplitudes, consts[0], consts[1])
+    )(held[0], pad, *held[1:])
 
     def field(size):
         return [
@@ -645,25 +631,19 @@
             VMEM((2, 2, size, h, wide // 4), f32),
             VMEM((2, size, h, wide), f32),
             VMEM((2, size, h, wide // 2), f32),
-            VMEM((2, 2, size, h, wide // 2), f32),
         ]
 
     step_size = 1.0 / math.sqrt(positions * n * 2)
-    return pl.pallas_call(
-        functools.partial(reduce_kernel, nx, ny, step_size),
+    core, light, total = pl.pallas_call(
+        functools.partial(reduce_kernel, nx, ny),
         out_shape=[
-            jax.ShapeDtypeStruct(specimen.shape, f32),
-            jax.ShapeDtypeStruct(probe_wave.shape, f32),
+            shaped((2, 2, 2, h, wide // 2), f32),
+            shaped((2, 2, 1, h, wide // 2), f32),
+            shaped((2, n, s, lanes), f32),
         ],
-        in_specs=[anywhere] * 4,
-        out_specs=[vm, vm],
+        in_specs=[vm] * 2,
+        out_specs=[vm, vm, vm],
         scratch_shapes=[
-            VMEM(specimen.shape, f32),
-            VMEM(probe_wave.shape, f32),
-            VMEM((4, 2, h, wide), f32),
-            VMEM((4, 1, h, wide), f32),
-            VMEM((n, s, lanes), f32),
-            VMEM((2, n, s, lanes), f32),
             *field(2),
             *field(1),
             VMEM((n, s, lanes), f32),
@@ -677,11 +657,21 @@
             dma((8,)),
             dma((6, most)),
             dma((6, most)),
-            dma((5,)),
         ],
-        compiler_params=pltpu.CompilerParams(collective_id=1, has_side_effects=True),
+        compiler_params=pltpu.CompilerParams(vmem_limit_bytes=32 * 2**20, collective_id=1, has_side_effects=True),
         name="reduce",
-    )(grad.reshape(3, 4, 2, h, wide), prob, specimen, probe_wave)
+    )(grad.reshape(3, 4, 2, h, wide), prob)
+    return pl.pallas_call(
+        functools.partial(apply_kernel, step_size),
+        out_shape=[
+            jax.ShapeDtypeStruct(specimen.shape, f32),
+            jax.ShapeDtypeStruct(probe_wave.shape, f32),
+        ],
+        in_specs=[vm] * 5,
+        out_specs=[vm, vm],
+        compiler_params=pltpu.CompilerParams(vmem_limit_bytes=16 * 2**20),
+        name="apply",
+    )(core, light, total, pad, held[1])
 
 
 def solution(mesh):

time: 51.2 us -> 42.6 us (0.83)
  Pallas kernels: 46.6 us -> 41.8 us
  local copies, waits for them, and re-layouts: 3.74 us -> 0 us
    unnamed x2 -> x0, local copies, waits for them, and re-layouts: 3.74 us -> none
    pallas_call x1, Pallas kernels: 8.2 us -> 4.8 us  [shards(): pl.pallas_call(step_kernel, out_shape=[jax.ShapeDtypeStruct((3, wide, wid...]
    pallas_call x2 -> x3, Pallas kernels: 38.4 us -> 37 us  [the longest x1 22.8 us: shards(): pl.pallas_call(functools.partial(reduce_kernel, nx, ny), out_shape=[shape...]
where the time goes in v3:
time: 42.6 us; the launch traced here: 42.5 us
  Pallas kernels  41.8 us (98%)
  between operations  0.65 us (2%)
    pallas_call x1, Pallas kernels, shards(): pl.pallas_call(functools.partial(reduce_kernel, nx, ny), out_shape=[shape...  22.8 us
    pallas_call x1, Pallas kernels, shards(): pl.pallas_call(functools.partial(halo_kernel, nx, ny), out_shape=[shaped(...  13.1 us
    pallas_call x1, Pallas kernels, shards(): pl.pallas_call(step_kernel, out_shape=[jax.ShapeDtypeStruct((3, wide, wid...  4.8 us
    pallas_call x1, Pallas kernels, shards(): pl.pallas_call(functools.partial(apply_kernel, step_size), out_shape=[jax...  1.14 us

profile of v3, /device:TPU:0, one launch (start us, length us, event | category | flops | bytes accessed | tf_op | source)
XLA Modules:
  0.0 42.5 jit_solution(14622753364608919350)
XLA Ops:
  0.6 13.1 %halo.1 = (f32[2,512,512]{2,1,0:T(8,128)S(1)}, s32[2,2]{1,0:T(2,128)S(1)}, f32[2,256,256]{2,1,0:T(8,128)S(1)}, bf16[2,256,256]{2,1,0:T(8,128)(2,1)S(1)}, bf16[51...) custom-call(f32[2,256,256]{2,1,0:T(8,128)} %spec.1, s32[2,2]{1,0:T(2,128)} %refs_0_.1, f32[2,256,256]{2,1,0:T(8,128)} %refs_1_.1, ...), custom_call_target="tpu_custom_call" | custom-call | tf_op jit(solution)/shard_map/halo/pallas_call | solution.py:605
  13.8 4.8 %step.1 = (f32[3,512,512]{2,1,0:T(8,128)S(1)}, f32[2,8,64,128]{3,2,1,0:T(8,128)S(1)}) custom-call(s32[2,2]{1,0:T(2,128)S(1)} %get-tuple-element.13.offsets, f32[2,512,512]{2,1,0:T(8,128)S(1)} %get-tuple-element.14.pad, f32[2,256,256]{2,1,0:T(8,128)S(1)} %get-tuple-element.15.probe, bf16[2,256,256]{2,1,0:T(8,128)(2,1)S(1)} %get-tuple-element.16.amplitudes, ...), custom_call_target="tpu_custom_call" | custom-call | tf_op jit(solution)/shard_map/step/pallas_call | solution.py:614
  18.6 22.8 %reduce.1 = (f32[2,2,2,64,256]{4,3,2,1,0:T(8,128)S(1)}, f32[2,2,1,64,256]{4,3,2,1,0:T(8,128)S(1)}, f32[2,8,64,128]{3,2,1,0:T(8,128)S(1)}) custom-call(f32[3,4,2,64,512]{4,3,2,1,0:T(8,128)S(1)} %bitcast.1, f32[2,8,64,128]{3,2,1,0:T(8,128)S(1)} %get-tuple-element.20.refs_1_), custom_call_target="tpu_custom_call" | custom-call | tf_op jit(solution)/shard_map/reduce/pallas_call | solution.py:637
  41.3 1.1 %apply.1 = (f32[2,256,256]{2,1,0:T(8,128)}, f32[2,256,256]{2,1,0:T(8,128)}) custom-call(f32[2,2,2,64,256]{4,3,2,1,0:T(8,128)S(1)} %get-tuple-element.21.core, f32[2,2,1,64,256]{4,3,2,1,0:T(8,128)S(1)} %get-tuple-element.22.light, f32[2,8,64,128]{3,2,1,0:T(8,128)S(1)} %get-tuple-element.23.total, f32[2,512,512]{2,1,0:T(8,128)S(1)} %get-tuple-element.14.pad, ...), custom_call_target="tpu_custom_call" | custom-call | tf_op jit(solution)/shard_map/apply/pallas_call | solution.py:664

commit v4 on v3

--- a/solution.py
+++ b/solution.py
@@ -525,28 +525,27 @@
         fold.add(0)
         fold.add(1)
         fold.send_rims(0)
-        light.add(0)
-        light.add(1)
+        fold.add(2)
+        for i in range(3):
+            light.add(i)
+        probe_sum.step2()
         light.send_rims(0)
-        fold.add(2)
-        light.add(2)
-        probe_sum.step2()
         fold.fold(0)
         fold.send_rims(1)
+        probe_sum.step3()
         light.fold(0)
         light.send_rims(1)
-        probe_sum.step3()
+        probe_sum.step4()
         fold.fold(1)
         fold.share()
         light.fold(1)
         light.share()
-        probe_sum.step4()
+        probe_sum.step5()
         light.arrive()
         fold.arrive()
 
     each(objects)
     def closing(q):
-        probes[q].step5()
         probes[1 - q].arrive()
         lights[q].finish()
         folds[q].finish()

time: 42.6 us -> 42.8 us (level)
  no operation moved by 1% of the time
where the time goes in v4:
time: 42.8 us; the launch traced here: 42.7 us
  Pallas kernels  42 us (98%)
  between operations  0.65 us (2%)
    pallas_call x1, Pallas kernels, shards(): pl.pallas_call(functools.partial(reduce_kernel, nx, ny), out_shape=[shape...  22.9 us
    pallas_call x1, Pallas kernels, shards(): pl.pallas_call(functools.partial(halo_kernel, nx, ny), out_shape=[shaped(...  13.1 us
    pallas_call x1, Pallas kernels, shards(): pl.pallas_call(step_kernel, out_shape=[jax.ShapeDtypeStruct((3, wide, wid...  4.8 us
    pallas_call x1, Pallas kernels, shards(): pl.pallas_call(functools.partial(apply_kernel, step_size), out_shape=[jax...  1.14 us

profile of v4, /device:TPU:0, one launch (start us, length us, event | category | flops | bytes accessed | tf_op | source)
XLA Modules:
  0.0 42.7 jit_solution(2439837554079889478)
XLA Ops:
  0.6 13.1 %halo.1 = (f32[2,512,512]{2,1,0:T(8,128)S(1)}, s32[2,2]{1,0:T(2,128)S(1)}, f32[2,256,256]{2,1,0:T(8,128)S(1)}, bf16[2,256,256]{2,1,0:T(8,128)(2,1)S(1)}, bf16[51...) custom-call(f32[2,256,256]{2,1,0:T(8,128)} %spec.1, s32[2,2]{1,0:T(2,128)} %refs_0_.1, f32[2,256,256]{2,1,0:T(8,128)} %refs_1_.1, ...), custom_call_target="tpu_custom_call" | custom-call | tf_op jit(solution)/shard_map/halo/pallas_call | solution.py:604
  13.8 4.8 %step.1 = (f32[3,512,512]{2,1,0:T(8,128)S(1)}, f32[2,8,64,128]{3,2,1,0:T(8,128)S(1)}) custom-call(s32[2,2]{1,0:T(2,128)S(1)} %get-tuple-element.13.offsets, f32[2,512,512]{2,1,0:T(8,128)S(1)} %get-tuple-element.14.pad, f32[2,256,256]{2,1,0:T(8,128)S(1)} %get-tuple-element.15.probe, bf16[2,256,256]{2,1,0:T(8,128)(2,1)S(1)} %get-tuple-element.16.amplitudes, ...), custom_call_target="tpu_custom_call" | custom-call | tf_op jit(solution)/shard_map/step/pallas_call | solution.py:613
  18.6 22.9 %reduce.1 = (f32[2,2,2,64,256]{4,3,2,1,0:T(8,128)S(1)}, f32[2,2,1,64,256]{4,3,2,1,0:T(8,128)S(1)}, f32[2,8,64,128]{3,2,1,0:T(8,128)S(1)}) custom-call(f32[3,4,2,64,512]{4,3,2,1,0:T(8,128)S(1)} %bitcast.1, f32[2,8,64,128]{3,2,1,0:T(8,128)S(1)} %get-tuple-element.20.refs_1_), custom_call_target="tpu_custom_call" | custom-call | tf_op jit(solution)/shard_map/reduce/pallas_call | solution.py:636
  41.5 1.1 %apply.1 = (f32[2,256,256]{2,1,0:T(8,128)}, f32[2,256,256]{2,1,0:T(8,128)}) custom-call(f32[2,2,2,64,256]{4,3,2,1,0:T(8,128)S(1)} %get-tuple-element.21.core, f32[2,2,1,64,256]{4,3,2,1,0:T(8,128)S(1)} %get-tuple-element.22.light, f32[2,8,64,128]{3,2,1,0:T(8,128)S(1)} %get-tuple-element.23.total, f32[2,512,512]{2,1,0:T(8,128)S(1)} %get-tuple-element.14.pad, ...), custom_call_target="tpu_custom_call" | custom-call | tf_op jit(solution)/shard_map/apply/pallas_call | solution.py:663

commit v5 on v4

--- a/solution.py
+++ b/solution.py
@@ -302,21 +302,22 @@
             out.append(self.copy(ref, ref, 3, d, {r.axis2: j}))
         return out
 
-    def gather1(self, back):
+    def gather1(self, e, back):
         r = self.r
         out = []
+        place = lax.rem(r.me2 - e + r.n2, r.n2)
         for d in range(1, r.n1):
             j = lax.rem(r.me1 + d, r.n1)
             origin = lax.rem(r.me1 - d + r.n1, r.n1) if back else r.me1
-            ref = self.total.at[r.q, pl.ds(origin * r.n2, r.n2)]
-            out.append(self.copy(ref, ref, 4, d, {r.axis1: j}))
+            ref = self.total.at[r.q, pl.ds(origin * r.n2 + place, 1)]
+            out.append(self.copy(ref, ref, 5 + e, d, {r.axis1: j}))
         return out
 
     def share_copy(self, d, sender):
         r = self.r
         origin = lax.rem(r.me1 - d + r.n1, r.n1)
         ref = self.total.at[r.q, pl.ds(origin * r.n2, r.n2)]
-        return self.copy(ref, ref, 5, d, self.partner)
+        return self.copy(ref, ref, 4, d, self.partner)
 
     def step1(self):
         self.pair_copy().wait_recv()
@@ -341,19 +342,21 @@
             c.wait_recv()
             one = one + self.pr2[d : d + 1]
         self.total[r.q, pl.ds(r.me1 * r.n2 + r.me2, 1)] = one
-        for c in self.gather2(0):
+        for c in self.gather2(0) + self.gather1(0, 0):
             c.start()
 
     def step4(self):
-        for c in self.gather2(1):
+        for e, c in enumerate(self.gather2(1), 1):
             c.wait_recv()
-        for c in self.gather1(0):
-            c.start()
+            for onward in self.gather1(e, 0):
+                onward.start()
         self.share_copy(0, True).start()
 
     def step5(self):
-        for d, c in enumerate(self.gather1(1), 1):
-            c.wait_recv()
+        landing = [self.gather1(e, 1) for e in range(self.r.n2)]
+        for d in range(1, self.r.n1):
+            for e in range(self.r.n2):
+                landing[e][d - 1].wait_recv()
             self.share_copy(d, True).start()
 
     def arrive(self):
@@ -362,8 +365,11 @@
 
     def finish(self):
         self.pair_copy().wait_send()
-        for c in self.scatter1() + self.scatter2() + self.gather2(0) + self.gather1(0):
+        for c in self.scatter1() + self.scatter2() + self.gather2(0):
             c.wait_send()
+        for e in range(self.r.n2):
+            for c in self.gather1(e, 0):
+                c.wait_send()
         for d in range(self.r.n1):
             self.share_copy(d, True).wait_send()
 
@@ -654,8 +660,8 @@
             dma((8,)),
             dma((8,)),
             dma((8,)),
-            dma((6, most)),
-            dma((6, most)),
+            dma((5 + most, most)),
+            dma((5 + most, most)),
         ],
         compiler_params=pltpu.CompilerParams(vmem_limit_bytes=32 * 2**20, collective_id=1, has_side_effects=True),
         name="reduce",

time: 42.8 us -> 43 us (level)
  no operation moved by 1% of the time
where the time goes in v5:
time: 43 us; the launch traced here: 42.9 us
  Pallas kernels  42.2 us (98%)
  between operations  0.65 us (2%)
    pallas_call x1, Pallas kernels, shards(): pl.pallas_call(functools.partial(reduce_kernel, nx, ny), out_shape=[shape...  23.2 us
    pallas_call x1, Pallas kernels, shards(): pl.pallas_call(functools.partial(halo_kernel, nx, ny), out_shape=[shaped(...  13.1 us
    pallas_call x1, Pallas kernels, shards(): pl.pallas_call(step_kernel, out_shape=[jax.ShapeDtypeStruct((3, wide, wid...  4.81 us
    pallas_call x1, Pallas kernels, shards(): pl.pallas_call(functools.partial(apply_kernel, step_size), out_shape=[jax...  1.14 us

profile of v5, /device:TPU:0, one launch (start us, length us, event | category | flops | bytes accessed | tf_op | source)
XLA Modules:
  0.0 42.9 jit_solution(10272896100493251185)
XLA Ops:
  0.6 13.1 %halo.1 = (f32[2,512,512]{2,1,0:T(8,128)S(1)}, s32[2,2]{1,0:T(2,128)S(1)}, f32[2,256,256]{2,1,0:T(8,128)S(1)}, bf16[2,256,256]{2,1,0:T(8,128)(2,1)S(1)}, bf16[51...) custom-call(f32[2,256,256]{2,1,0:T(8,128)} %spec.1, s32[2,2]{1,0:T(2,128)} %refs_0_.1, f32[2,256,256]{2,1,0:T(8,128)} %refs_1_.1, ...), custom_call_target="tpu_custom_call" | custom-call | tf_op jit(solution)/shard_map/halo/pallas_call | solution.py:610
  13.8 4.8 %step.1 = (f32[3,512,512]{2,1,0:T(8,128)S(1)}, f32[2,8,64,128]{3,2,1,0:T(8,128)S(1)}) custom-call(s32[2,2]{1,0:T(2,128)S(1)} %get-tuple-element.13.offsets, f32[2,512,512]{2,1,0:T(8,128)S(1)} %get-tuple-element.14.pad, f32[2,256,256]{2,1,0:T(8,128)S(1)} %get-tuple-element.15.probe, bf16[2,256,256]{2,1,0:T(8,128)(2,1)S(1)} %get-tuple-element.16.amplitudes, ...), custom_call_target="tpu_custom_call" | custom-call | tf_op jit(solution)/shard_map/step/pallas_call | solution.py:619
  18.6 23.2 %reduce.1 = (f32[2,2,2,64,256]{4,3,2,1,0:T(8,128)S(1)}, f32[2,2,1,64,256]{4,3,2,1,0:T(8,128)S(1)}, f32[2,8,64,128]{3,2,1,0:T(8,128)S(1)}) custom-call(f32[3,4,2,64,512]{4,3,2,1,0:T(8,128)S(1)} %bitcast.1, f32[2,8,64,128]{3,2,1,0:T(8,128)S(1)} %get-tuple-element.20.refs_1_), custom_call_target="tpu_custom_call" | custom-call | tf_op jit(solution)/shard_map/reduce/pallas_call | solution.py:642
  41.8 1.1 %apply.1 = (f32[2,256,256]{2,1,0:T(8,128)}, f32[2,256,256]{2,1,0:T(8,128)}) custom-call(f32[2,2,2,64,256]{4,3,2,1,0:T(8,128)S(1)} %get-tuple-element.21.core, f32[2,2,1,64,256]{4,3,2,1,0:T(8,128)S(1)} %get-tuple-element.22.light, f32[2,8,64,128]{3,2,1,0:T(8,128)S(1)} %get-tuple-element.23.total, f32[2,512,512]{2,1,0:T(8,128)S(1)} %get-tuple-element.14.pad, ...), custom_call_target="tpu_custom_call" | custom-call | tf_op jit(solution)/shard_map/apply/pallas_call | solution.py:669
